TPU v7x, 32 devices: a whole 2x2x4 slice. The times are simulated.
32 devices in a mesh: gx: 8 (over z, y), gy: 4 (over x, core).
Axes of the slice: x: 2, y: 2, z: 4, core: 2. Of those that a mesh axis runs over, the one named last changes fastest.
Arguments:
- point_feats: bfloat16 [32, 262144], P(None, ('gx', 'gy')), may hold values from -1 to 1
- point_targets: bfloat16 [262144], P(('gx', 'gy')), may hold values from -6 to 6
- point_lists: int32 [32768, 8], P(('gx', 'gy')), may hold values from -1 to 8191, as said below
- brick_adjacency: int32 [1024, 4], P(('gx', 'gy')), may hold values from -1 to 1023, as said below
- voxel_feats: float32 [1024, 32, 512], P(('gx', 'gy')), may hold values from -0.25 to 0.25
- voxel_reg: float32 [1024, 512], P(('gx', 'gy')), may hold values from 0.25 to 2
Outputs:
- solution: float32 [1024, 512], P(('gx', 'gy'))
- residual: float32 [1024, 512], P(('gx', 'gy'))
Inputs may be any that keep to these rules, and one draw needn't show every extreme that they name: `point_lists`: row s * 1024 + b lists, in its first slots, distinct indices of the points of source device s in brick b, all within that device's rows b * 8 to b * 8 + 7, then -1 in the remaining slots. Point rows named by no list are unused. `brick_adjacency`: entry k of brick b is the lattice neighbour of b in direction k (minus along the road, plus along the road, minus across, plus across) or -1; the relation is symmetric and -1 wherever the neighbour lies outside the lattice.
All inputs are finite; a program needn't handle non-finite values.
Results may differ from a plain program's by a relative error of at most 0.0003.
Values may be sent and summed in bfloat16 or wider, within the bound.
A program may use at most 64 MiB of HBM per device.

v0:
```python
import functools
import math

import jax
import jax.numpy as jnp
from jax import lax
from jax.experimental import pallas as pl
from jax.experimental.pallas import tpu as pltpu
from jax.sharding import PartitionSpec as P

BX = 8
BY = 4
ITERS = 3
LANES = 128
CHUNK = 8
MESH = pl.DeviceIdType.MESH
STRIDE = 11
SCALE = 2.0**-8
SHIFTS = (8.0, 1.0, 4.0)

coupling_weight = 1.0


def kernel(
    gx,
    gy,
    feats_hbm,
    target_ref,
    lists_ref,
    adjacency_ref,
    voxel_hbm,
    reg_ref,
    answer_ref,
    res_ref,
    direction_ref,
    image_ref,
    alpha_ref,
    got,
    got_extra,
    extra,
    flat,
    voxel,
    acc,
    square,
    basis,
    z_ref,
    q_ref,
    my_ref,
    mid_ref,
    ym_ref,
    yp_ref,
    y_send,
    halo,
    part,
    parts,
    voxel_sem,
    feat_send,
    feat_recv,
    extra_send,
    extra_recv,
    halo_send,
    halo_recv,
    part_send,
    part_recv,
):
    count = gx * gy
    ix, iy = lax.axis_index("gx"), lax.axis_index("gy")
    me = ix * gy + iy
    feat, cols = got.shape[1], got.shape[2]
    bricks = reg_ref.shape[0]
    slots = cols // bricks
    halves = cols // LANES
    per_half = LANES // slots

    step_by = STRIDE if math.gcd(STRIDE, count) == 1 else 1

    def place(index):
        return (index // gy, index % gy)

    barrier = pltpu.get_barrier_semaphore()

    def greet(j, _):
        pl.semaphore_signal(
            barrier, inc=1, device_id=place((me + j * step_by) % count), device_id_type=MESH
        )
        return 0

    lax.fori_loop(1, count, greet, 0, unroll=True)
    voxel_copy = pltpu.make_async_copy(voxel_hbm, voxel, voxel_sem)
    voxel_copy.start()
    halo[...] = jnp.zeros_like(halo)
    acc[...] = jnp.zeros_like(acc)
    own_feat = pltpu.make_async_copy(
        feats_hbm.at[:, pl.ds(pl.multiple_of(me * cols, cols), cols)], got.at[me], feat_recv.at[me]
    )
    own_extra = pltpu.make_async_copy(extra.at[me], got_extra.at[me], extra_recv.at[me])
    own_feat.start()

    total_bricks = lists_ref.shape[1]
    groups = total_bricks // LANES
    wide = slots * LANES
    listed = lists_ref[...]
    offset = listed - slots * lax.broadcasted_iota(jnp.int32, listed.shape, 1)
    offset = jnp.where(listed >= 0, offset, -1)
    hits = jnp.concatenate(
        [
            jnp.max(jnp.where(offset == d, 1.0, 0.0), axis=0, keepdims=True)
            for d in range(slots)
        ],
        axis=0,
    )
    hits = jnp.concatenate(
        [hits[:, g * LANES : (g + 1) * LANES] for g in range(groups)], axis=0
    ).astype(jnp.bfloat16)
    spread = jnp.where(
        lax.broadcasted_iota(jnp.int32, (LANES, wide), 1) // slots
        == lax.broadcasted_iota(jnp.int32, (LANES, wide), 0),
        1.0,
        0.0,
    ).astype(jnp.bfloat16)
    spread_hits = jnp.dot(hits, spread, preferred_element_type=jnp.float32)
    same = (
        lax.broadcasted_iota(jnp.int32, (slots, wide), 1) % slots
        == lax.broadcasted_iota(jnp.int32, (slots, wide), 0)
    )
    live_rows = jnp.sum(
        jnp.where(same[None], spread_hits.reshape(groups, slots, wide), 0.0), axis=1
    )
    for l in range(slots):
        flat[pl.ds(l, groups, stride=slots), :] = live_rows[:, l * LANES : (l + 1) * LANES]
    targets = target_ref[...].astype(jnp.float32)
    for k in range(count):
        rows = slice(k * halves, (k + 1) * halves)
        extra[k] = jnp.concatenate([flat[rows, :], targets[rows]], axis=0).astype(jnp.bfloat16)
    own_extra.start()
    pl.semaphore_wait(barrier, count - 1)

    def feat_copy(to, frm):
        return pltpu.make_async_remote_copy(
            src_ref=feats_hbm.at[:, pl.ds(pl.multiple_of(to * cols, cols), cols)],
            dst_ref=got.at[frm],
            send_sem=feat_send.at[to],
            recv_sem=feat_recv.at[frm],
            device_id=place(to),
            device_id_type=MESH,
        )

    def extra_copy(to, frm):
        return pltpu.make_async_remote_copy(
            src_ref=extra.at[to],
            dst_ref=got_extra.at[frm],
            send_sem=extra_send.at[to],
            recv_sem=extra_recv.at[frm],
            device_id=place(to),
            device_id_type=MESH,
        )

    def send(j, _):
        to = (me + j * step_by) % count
        feat_copy(to, me).start()
        extra_copy(to, me).start()
        return 0

    lax.fori_loop(1, count, send, 0)
    voxel_copy.wait()
    square[...] = jnp.zeros_like(square)

    def squares(t, _):
        for u in range(4):
            b = t * 4 + u
            rows = pl.ds(pl.multiple_of(b * feat, feat), feat)
            square[rows, 0:feat] = lax.dot_general(
                voxel[b],
                voxel[b],
                (((1,), (1,)), ((), ())),
                precision=lax.Precision.HIGHEST,
                preferred_element_type=jnp.float32,
            )
        return 0

    lax.fori_loop(0, bricks // 4, squares, 0)
    own_feat.wait()
    own_extra.wait()

    group = 4
    while count % group:
        group //= 2
    lane = lax.broadcasted_iota(jnp.int32, (1, group * LANES), 1)
    owner = (lane // slots) % per_half

    def absorb(g, _):
        sources = []
        for u in range(group):
            j = g * group + u
            source = (me + (count - j) * step_by) % count
            sources.append(source)
            if u:
                feat_copy(source, source).wait_recv()
                extra_copy(source, source).wait_recv()
            else:

                @pl.when(g > 0)
                def _():
                    feat_copy(source, source).wait_recv()
                    extra_copy(source, source).wait_recv()

        for h in range(halves):
            span = slice(h * LANES, (h + 1) * LANES)
            x = jnp.concatenate([got[s, :, span] for s in sources], axis=1)
            more = jnp.concatenate(
                [got_extra[s].astype(jnp.float32) for s in sources], axis=1
            )
            live = more[h : h + 1]
            target = more[halves + h : halves + h + 1].astype(jnp.bfloat16)
            left = jnp.concatenate(
                [x * jnp.where(owner == b, live, 0.0).astype(jnp.bfloat16) for b in range(per_half)],
                axis=0,
            )
            right = jnp.concatenate(
                [
                    x,
                    jnp.broadcast_to(target, (16, group * LANES)),
                    jnp.zeros((LANES - feat - 16, group * LANES), jnp.bfloat16),
                ],
                axis=0,
            )
            rows = slice(h * per_half * feat, (h + 1) * per_half * feat)
            acc[rows, :] += lax.dot_general(
                left, right, (((1,), (1,)), ((), ())), preferred_element_type=jnp.float32
            )
        return 0

    lax.fori_loop(0, count // group, absorb, 0)

    eye = lax.broadcasted_iota(jnp.int32, (1, feat, LANES), 1) == lax.broadcasted_iota(
        jnp.int32, (1, feat, LANES), 2
    )
    chunks = bricks // CHUNK
    in_feat = lax.broadcasted_iota(jnp.int32, (bricks, LANES), 1) < feat

    def at(t):
        return pl.ds(pl.multiple_of(t * CHUNK, CHUNK), CHUNK)

    def block(ref, t):
        rows = pl.ds(pl.multiple_of(t * CHUNK * feat, CHUNK * feat), CHUNK * feat)
        return ref[rows, :].reshape(CHUNK, feat, LANES)

    def as_column(rows):
        return jnp.sum(jnp.where(eye, rows[:, None, :], 0.0), axis=2, keepdims=True)

    def gathered(t):
        return block(acc, t)[:, :, feat : feat + 1]

    def begin(t, _):
        z_ref[0, at(t), :] = jnp.sum(block(square, t) * gathered(t), axis=1)
        return 0

    lax.fori_loop(0, chunks, begin, 0, unroll=True)

    linked = jnp.where(adjacency_ref[...] >= 0, 1.0, 0.0)
    same_brick = lax.broadcasted_iota(jnp.int32, (bricks, bricks), 0) == lax.broadcasted_iota(
        jnp.int32, (bricks, bricks), 1
    )
    weights = [
        jnp.sum(jnp.where(same_brick, linked[k : k + 1], 0.0), axis=1, keepdims=True)
        for k in range(4)
    ]
    masks = [w > 0.0 for w in weights]
    degree = weights[0] + weights[1] + weights[2] + weights[3]
    here = [ix > 0, ix < gx - 1, iy > 0, iy < gy - 1]
    beside = [(ix - 1, iy), (ix + 1, iy), (ix, iy - 1), (ix, iy + 1)]

    def halo_copy(step, k):
        if k < 2:
            source = z_ref.at[step, pl.ds(k * (bricks - 8), 8)]
        else:
            source = y_send.at[step, k - 2]
        return pltpu.make_async_remote_copy(
            src_ref=source,
            dst_ref=halo.at[step, k ^ 1],
            send_sem=halo_send.at[step, k],
            recv_sem=halo_recv.at[step, k ^ 1],
            device_id=beside[k],
            device_id_type=MESH,
        )

    def halo_arrived(step, k):
        return pltpu.make_async_remote_copy(
            src_ref=y_send.at[step, 0],
            dst_ref=halo.at[step, k],
            send_sem=halo_send.at[step, k],
            recv_sem=halo_recv.at[step, k],
            device_id=beside[k],
            device_id_type=MESH,
        )

    def part_copy(to, frm):
        return pltpu.make_async_remote_copy(
            src_ref=part,
            dst_ref=parts.at[frm],
            send_sem=part_send.at[to],
            recv_sem=part_recv.at[frm],
            device_id=place(to),
            device_id_type=MESH,
        )

    def fold(values):
        total = jnp.sum(values, axis=0, keepdims=True)
        width = total.shape[1]
        return sum(total[:, c : c + LANES] for c in range(0, width, LANES))

    def next_basis(step, t):
        if step == 0:
            return jnp.sum(voxel[at(t)] * gathered(t), axis=1)
        back = jnp.sum(voxel[at(t)] * as_column(mid_ref[at(t), :]), axis=1)
        shifted = (reg_ref[at(t), :] - SHIFTS[step - 1]) * basis[step - 1, at(t), :]
        return SCALE * (back + shifted)

    def operate(step):
        for e in range(2):
            y_send[step, e] = z_ref[step, pl.ds(e * (BY - 1), BX, stride=BY), :]
        for k in range(4):

            @pl.when(here[k])
            def _():
                halo_copy(step, k).start()

        def widen(t, _):
            made = next_basis(step, t)
            basis[step, at(t), :] = made
            if step + 1 < ITERS:
                weighted = reg_ref[at(t), :] * made
                column = jnp.sum(voxel[at(t)] * weighted[:, None, :], axis=2, keepdims=True)
                q_ref[at(t), :] = jnp.sum(jnp.where(eye, column, 0.0), axis=1)
            my_ref[at(t), :] = jnp.sum(block(acc, t) * as_column(z_ref[step, at(t), :]), axis=1)
            return 0

        lax.fori_loop(0, chunks, widen, 0)
        z = z_ref[step]
        ym_ref[1:bricks, :] = z[: bricks - 1]
        yp_ref[0 : bricks - 1, :] = z[1:]
        found = []
        if step + 1 == ITERS:
            found = [fold(basis[a] * basis[b]) for a, b in early]
            final = (reg_ref[...] - SHIFTS[step]) * basis[step]
            found = found + [fold(basis[a] * final) for a, b in late]
        for k in range(4):

            @pl.when(here[k])
            def _():
                halo_arrived(step, k).wait_recv()

        xm = jnp.concatenate([halo[step, 0][8 - BY :], z[: bricks - BY]], axis=0)
        xp = jnp.concatenate([z[BY:], halo[step, 1][:BY]], axis=0)
        ym_ref[pl.ds(0, BX, stride=BY), :] = halo[step, 2]
        yp_ref[pl.ds(BY - 1, BX, stride=BY), :] = halo[step, 3]
        near = jnp.where(masks[0], xm, 0.0) + jnp.where(masks[1], xp, 0.0)
        near = near + jnp.where(masks[2], ym_ref[...], 0.0) + jnp.where(masks[3], yp_ref[...], 0.0)
        mid = jnp.where(in_feat, my_ref[...] + coupling_weight * (degree * z - near), 0.0)
        mid_ref[...] = mid

        if step + 1 < ITERS:

            def advance(t, _):
                back = jnp.sum(block(square, t) * as_column(mid_ref[at(t), :]), axis=1)
                shifted = q_ref[at(t), :] - SHIFTS[step] * z_ref[step, at(t), :]
                z_ref[step + 1, at(t), :] = SCALE * (back + shifted)
                return 0

            lax.fori_loop(0, chunks, advance, 0, unroll=True)
        else:
            for e, (a, b) in enumerate(late):
                e += len(early)
                found[e] = SCALE * (found[e] + fold(z_ref[a] * mid))
        return found

    early = [(a, b) for a in range(ITERS) for b in range(a, ITERS)]
    late = [(a, ITERS) for a in range(ITERS)]
    pairs = early + late
    rows = []
    for step in range(ITERS):
        rows = operate(step)
    rows = rows + [jnp.zeros_like(rows[0])] * (-len(rows) % 8)
    sums = jnp.sum(jnp.concatenate(rows, axis=0), axis=1, keepdims=True)
    entry = lax.broadcasted_iota(jnp.int32, (len(rows), LANES), 1)
    diagonal = entry == lax.broadcasted_iota(jnp.int32, (len(rows), LANES), 0)
    mine = jnp.sum(jnp.where(diagonal, sums, 0.0), axis=0, keepdims=True)
    part[...] = mine
    parts[me] = mine

    def start(j, _):
        part_copy((me + j * step_by) % count, me).start()
        return 0

    lax.fori_loop(1, count, start, 0, unroll=True)

    def last(t, _):
        basis[ITERS, at(t), :] = next_basis(ITERS, t)
        return 0

    lax.fori_loop(0, chunks, last, 0)

    def finish(j, _):
        source = (me + (count - j) * step_by) % count
        part_copy(source, source).wait_recv()
        return 0

    lax.fori_loop(1, count, finish, 0)
    total = jnp.sum(parts[...], axis=0)
    spread_total = jnp.sum(
        jnp.where(diagonal, jnp.broadcast_to(total, diagonal.shape), 0.0), axis=1, keepdims=True
    )
    gram = {}
    for e, (a, b) in enumerate(pairs):
        gram[a, b] = gram[b, a] = spread_total[e : e + 1]

    def inner(left, right):
        terms = [
            left[a] * right[b] * gram[a, b] for a in range(len(left)) for b in range(len(right))
        ]
        return functools.reduce(lambda p, q: p + q, terms)

    def apply(coefficients):
        size = len(coefficients)
        out = [SHIFTS[k] * coefficients[k] for k in range(size)]
        out.append(coefficients[-1] * (1.0 / SCALE))
        for k in range(1, size):
            out[k] = out[k] + coefficients[k - 1] * (1.0 / SCALE)
        return out

    one = jnp.ones((1, 1), jnp.float32)
    res, direction, answer = [one], [one], []
    norm_now = gram[0, 0]
    for step in range(ITERS):
        before_answer, before_res = answer, res
        image = apply(direction)
        alpha = norm_now / inner(direction, image)
        padded = answer + [jnp.zeros_like(one)] * (len(direction) - len(answer))
        answer = [p + alpha * d for p, d in zip(padded, direction)]
        res = [p - alpha * w for p, w in zip(res + [jnp.zeros_like(one)], image)]
        if step + 1 < ITERS:
            norm_next = inner(res, res)
            ratio = norm_next / norm_now
            direction = [
                p + ratio * d for p, d in zip(res, direction + [jnp.zeros_like(one)])
            ]
            norm_now = norm_next
    def combine(coefficients):
        return functools.reduce(
            lambda p, q: p + q, [c * basis[k] for k, c in enumerate(coefficients)]
        )

    answer_ref[...] = combine(before_answer)
    res_ref[...] = combine(before_res)
    direction_ref[...] = combine(direction)
    image_ref[...] = combine(image)
    alpha_ref[...] = jnp.broadcast_to(alpha, alpha_ref.shape)

    def drain(j, _):
        to = (me + j * step_by) % count
        feat_copy(to, me).wait_send()
        extra_copy(to, me).wait_send()
        part_copy(to, me).wait_send()
        return 0

    lax.fori_loop(1, count, drain, 0)
    for step in range(ITERS):
        for k in range(4):

            @pl.when(here[k])
            def _():
                halo_copy(step, k).wait_send()


def shards(gx, gy, point_feats, point_targets, point_lists, brick_adjacency, voxel_feats, voxel_reg):
    feat = point_feats.shape[0]
    brick_total, slots = point_lists.shape
    bricks, _, vox = voxel_feats.shape
    count = gx * gy
    cols = bricks * slots
    vmem = pl.BlockSpec(memory_space=pltpu.VMEM)
    hbm = pl.BlockSpec(memory_space=pl.ANY)
    f32 = jnp.float32
    answer, res, direction, image, alpha = pl.pallas_call(
        functools.partial(kernel, gx, gy),
        out_shape=(jax.ShapeDtypeStruct((bricks, vox), f32),) * 4
        + (jax.ShapeDtypeStruct((1, vox), f32),),
        in_specs=[hbm, vmem, vmem, vmem, hbm, vmem],
        out_specs=(vmem,) * 5,
        scratch_shapes=[
            pltpu.VMEM((count, feat, cols), jnp.bfloat16),
            pltpu.VMEM((count, 2 * cols // LANES, LANES), jnp.bfloat16),
            pltpu.VMEM((count, 2 * cols // LANES, LANES), jnp.bfloat16),
            pltpu.VMEM((count * cols // LANES, LANES), f32),
            pltpu.VMEM((bricks, feat, vox), f32),
            pltpu.VMEM((bricks * feat, LANES), f32),
            pltpu.VMEM((bricks * feat, LANES), f32),
            pltpu.VMEM((ITERS + 1, bricks, vox), f32),
            pltpu.VMEM((ITERS, bricks, LANES), f32),
            pltpu.VMEM((bricks, LANES), f32),
            pltpu.VMEM((bricks, LANES), f32),
            pltpu.VMEM((bricks, LANES), f32),
            pltpu.VMEM((bricks, LANES), f32),
            pltpu.VMEM((bricks, LANES), f32),
            pltpu.VMEM((ITERS, 2, BX, LANES), f32),
            pltpu.VMEM((ITERS, 4, 8, LANES), f32),
            pltpu.VMEM((1, LANES), f32),
            pltpu.VMEM((count, 1, LANES), f32),
            pltpu.SemaphoreType.DMA,
            pltpu.SemaphoreType.DMA((count,)),
            pltpu.SemaphoreType.DMA((count,)),
            pltpu.SemaphoreType.DMA((count,)),
            pltpu.SemaphoreType.DMA((count,)),
            pltpu.SemaphoreType.DMA((ITERS, 4)),
            pltpu.SemaphoreType.DMA((ITERS, 4)),
            pltpu.SemaphoreType.DMA((count,)),
            pltpu.SemaphoreType.DMA((count,)),
        ],
        compiler_params=pltpu.CompilerParams(collective_id=0, has_side_effects=True),
    )(
        point_feats,
        point_targets.reshape(-1, LANES),
        point_lists.T,
        brick_adjacency.T,
        voxel_feats,
        voxel_reg,
    )
    return answer + alpha * direction, res - alpha * image


def solution(mesh):
    placed = (
        P(None, ("gx", "gy")),
        P(("gx", "gy")),
        P(("gx", "gy"), None),
        P(("gx", "gy"), None),
        P(("gx", "gy"), None, None),
        P(("gx", "gy"), None),
    )
    return jax.shard_map(
        functools.partial(shards, mesh.shape["gx"], mesh.shape["gy"]),
        mesh=mesh,
        in_specs=placed,
        out_specs=(P(("gx", "gy"), None), P(("gx", "gy"), None)),
        check_vma=False,
    )
```

profile of v0, /device:TPU:0, one launch (start us, length us, event | category | flops | bytes accessed | tf_op | source)
XLA Modules:
  0.0 42.1 jit_solution(5193968909324050454)
XLA Ops:
  0.6 39.8 %shard_map.77 = (f32[32,512]{1,0:T(8,128)}, f32[32,512]{1,0:T(8,128)}, f32[32,512]{1,0:T(8,128)}, f32[32,512]{1,0:T(8,128)}, f32[1,512]{1,0:T(1,128)}) custom-call(bf16[32,8192]{1,0:T(8,128)(2,1)} %feats_hbm.1, bf16[64,128]{1,0:T(8,128)(2,1)} %bitcast.5, s32[8,1024]{1,0:T(8,128)} %bitcast.4, s32[4,32]{1,0:T(4,128)} %bitcast.6, f32[32,32,512]{2,1,0:T(8,128)} %voxel_hbm.1, ...), custom_call_target="tpu_custom_call" | custom-call | tf_op jit(solution)/shard_map/pallas_call | solution.py:484
  40.5 1.6 %multiply_subtract_fusion = (f32[32,512]{1,0:T(8,128)}, f32[32,512]{1,0:T(8,128)}) fusion(f32[32,512]{1,0:T(8,128)} %get-tuple-element.10, f32[32,512]{1,0:T(8,128)} %get-tuple-element.11, f32[512]{0:T(512)} %bitcast.7, f32[32,512]{1,0:T(8,128)} %get-tuple-element.7, f32[32,512]{1,0:T(8,128)} %get-tuple-element.9), kind=kLoop, calls=%fused_computation | loop fusion | flops 65536 | bytes 395264 | tf_op jit(solution)/shard_map/sub | solution.py:528
where the time goes:
time: 42.3 us; the launch traced here: 42.1 us
  Pallas kernels  39.8 us (94%)
  other arithmetic  1.6 us (4%)
  between operations  0.64 us (2%)
    pallas_call x1, Pallas kernels, shards(): pl.pallas_call(functools.partial(kernel, gx, gy), out_shape=(jax.ShapeDty...  39.8 us
    sub x1, other arithmetic, shards(): return (answer + alpha * direction, res - alpha * image)  1.6 us

commit v1 on v0

--- a/solution.py
+++ b/solution.py
@@ -25,11 +25,11 @@
     gx,
     gy,
     feats_hbm,
-    target_ref,
-    lists_ref,
-    adjacency_ref,
+    target_hbm,
+    lists_hbm,
+    adjacency_hbm,
     voxel_hbm,
-    reg_ref,
+    reg_hbm,
     answer_ref,
     res_ref,
     direction_ref,
@@ -53,7 +53,12 @@
     halo,
     part,
     parts,
+    target_ref,
+    lists_ref,
+    adjacency_ref,
+    reg_ref,
     voxel_sem,
+    input_sem,
     feat_send,
     feat_recv,
     extra_send,
@@ -86,6 +91,19 @@
         return 0
 
     lax.fori_loop(1, count, greet, 0, unroll=True)
+    inputs = [
+        pltpu.make_async_copy(source, target, input_sem.at[e])
+        for e, (source, target) in enumerate(
+            [
+                (lists_hbm, lists_ref),
+                (target_hbm, target_ref),
+                (reg_hbm, reg_ref),
+                (adjacency_hbm, adjacency_ref),
+            ]
+        )
+    ]
+    for copy in inputs:
+        copy.start()
     voxel_copy = pltpu.make_async_copy(voxel_hbm, voxel, voxel_sem)
     voxel_copy.start()
     halo[...] = jnp.zeros_like(halo)
@@ -99,6 +117,7 @@
     total_bricks = lists_ref.shape[1]
     groups = total_bricks // LANES
     wide = slots * LANES
+    inputs[0].wait()
     listed = lists_ref[...]
     offset = listed - slots * lax.broadcasted_iota(jnp.int32, listed.shape, 1)
     offset = jnp.where(listed >= 0, offset, -1)
@@ -128,6 +147,7 @@
     )
     for l in range(slots):
         flat[pl.ds(l, groups, stride=slots), :] = live_rows[:, l * LANES : (l + 1) * LANES]
+    inputs[1].wait()
     targets = target_ref[...].astype(jnp.float32)
     for k in range(count):
         rows = slice(k * halves, (k + 1) * halves)
@@ -163,6 +183,8 @@
 
     lax.fori_loop(1, count, send, 0)
     voxel_copy.wait()
+    inputs[2].wait()
+    inputs[3].wait()
     square[...] = jnp.zeros_like(square)
 
     def squares(t, _):
@@ -479,13 +501,12 @@
     count = gx * gy
     cols = bricks * slots
     vmem = pl.BlockSpec(memory_space=pltpu.VMEM)
-    hbm = pl.BlockSpec(memory_space=pl.ANY)
+    hbm = pl.BlockSpec(memory_space=pltpu.HBM)
     f32 = jnp.float32
     answer, res, direction, image, alpha = pl.pallas_call(
         functools.partial(kernel, gx, gy),
-        out_shape=(jax.ShapeDtypeStruct((bricks, vox), f32),) * 4
-        + (jax.ShapeDtypeStruct((1, vox), f32),),
-        in_specs=[hbm, vmem, vmem, vmem, hbm, vmem],
+        out_shape=(pltpu.VMEM((bricks, vox), f32),) * 4 + (pltpu.VMEM((1, vox), f32),),
+        in_specs=[hbm] * 6,
         out_specs=(vmem,) * 5,
         scratch_shapes=[
             pltpu.VMEM((count, feat, cols), jnp.bfloat16),
@@ -506,7 +527,12 @@
             pltpu.VMEM((ITERS, 4, 8, LANES), f32),
             pltpu.VMEM((1, LANES), f32),
             pltpu.VMEM((count, 1, LANES), f32),
+            pltpu.VMEM((count * cols // LANES, LANES), point_targets.dtype),
+            pltpu.VMEM((slots, brick_total), jnp.int32),
+            pltpu.VMEM((4, bricks), jnp.int32),
+            pltpu.VMEM((bricks, vox), f32),
             pltpu.SemaphoreType.DMA,
+            pltpu.SemaphoreType.DMA((4,)),
             pltpu.SemaphoreType.DMA((count,)),
             pltpu.SemaphoreType.DMA((count,)),
             pltpu.SemaphoreType.DMA((count,)),
@@ -516,14 +542,19 @@
             pltpu.SemaphoreType.DMA((count,)),
             pltpu.SemaphoreType.DMA((count,)),
         ],
-        compiler_params=pltpu.CompilerParams(collective_id=0, has_side_effects=True),
+        compiler_params=pltpu.CompilerParams(collective_id=0, has_side_effects=True, vmem_limit_bytes=16 * 1024 * 1024),
     )(
-        point_feats,
-        point_targets.reshape(-1, LANES),
-        point_lists.T,
-        brick_adjacency.T,
-        voxel_feats,
-        voxel_reg,
+        *(
+            pltpu.with_memory_space_constraint(x, pltpu.HBM)
+            for x in (
+                point_feats,
+                point_targets.reshape(-1, LANES),
+                point_lists.T,
+                brick_adjacency.T,
+                voxel_feats,
+                voxel_reg,
+            )
+        )
     )
     return answer + alpha * direction, res - alpha * image
 

time: 42.3 us -> 40 us (0.946)
  Pallas kernels: 39.8 us -> 38.5 us
  other arithmetic: 1.6 us -> 0.67 us
    pallas_call x1, Pallas kernels: 39.8 us -> 38.5 us  [shards(): pl.pallas_call(functools.partial(kernel, gx, gy), out_shape=(pltpu.VMEM((...]
    sub x1, other arithmetic: 1.6 us -> 0.67 us  [shards(): return (answer + alpha * direction, res - alpha * image)]
where the time goes in v1:
time: 40 us; the launch traced here: 39.9 us
  Pallas kernels  38.5 us (96%)
  other arithmetic  0.67 us (2%)
  between operations  0.64 us (2%)
    pallas_call x1, Pallas kernels, shards(): pl.pallas_call(functools.partial(kernel, gx, gy), out_shape=(pltpu.VMEM((...  38.5 us

profile of v1, /device:TPU:0, one launch (start us, length us, event | category | flops | bytes accessed | tf_op | source)
XLA Modules:
  0.0 39.9 jit_solution(11480420163286980899)
XLA Ops:
  0.6 38.5 %shard_map.77 = (f32[32,512]{1,0:T(8,128)S(1)}, f32[32,512]{1,0:T(8,128)S(1)}, f32[32,512]{1,0:T(8,128)S(1)}, f32[32,512]{1,0:T(8,128)S(1)}, f32[1,512]{1,0:T(1,128)S(1)}) custom-call(bf16[32,8192]{1,0:T(8,128)(2,1)} %feats_hbm.1, bf16[64,128]{1,0:T(8,128)(2,1)} %bitcast.6, s32[8,1024]{1,0:T(8,128)} %bitcast.5, s32[4,32]{1,0:T(4,128)} %bitcast.7, ...), custom_call_target="tpu_custom_call" | custom-call | tf_op jit(solution)/shard_map/pallas_call | solution.py:506
  39.2 0.7 %multiply_subtract_fusion = (f32[32,512]{1,0:T(8,128)}, f32[32,512]{1,0:T(8,128)}) fusion(f32[32,512]{1,0:T(8,128)S(1)} %get-tuple-element.10, f32[32,512]{1,0:T(8,128)S(1)} %get-tuple-element.11, f32[512]{0:T(512)S(1)} %bitcast.4, f32[32,512]{1,0:T(8,128)S(1)} %get-tuple-element.7, f32[32,512]{1,0:T(8,128)S(1)} %get-tuple-element.9), kind=kLoop, calls=%fused_computation | loop fusion | flops 65536 | bytes 395264 | tf_op jit(solution)/shard_map/sub | solution.py:559

commit v2 on v1

--- a/solution.py
+++ b/solution.py
@@ -16,6 +16,7 @@
 MESH = pl.DeviceIdType.MESH
 STRIDE = 11
 SCALE = 2.0**-8
+AHEAD = 8
 SHIFTS = (8.0, 1.0, 4.0)
 
 coupling_weight = 1.0
@@ -41,6 +42,9 @@
     flat,
     voxel,
     acc,
+    gather,
+    mz_ref,
+    g_ref,
     square,
     basis,
     z_ref,
@@ -76,18 +80,24 @@
     slots = cols // bricks
     halves = cols // LANES
     per_half = LANES // slots
+    side = LANES // feat
+    tall = per_half // side
 
     step_by = STRIDE if math.gcd(STRIDE, count) == 1 else 1
 
     def place(index):
         return (index // gy, index % gy)
 
+    def at_offset(j):
+        return (me + j * step_by) % count
+
+    def columns(index):
+        return pl.ds(pl.multiple_of(index * cols, cols), cols)
+
     barrier = pltpu.get_barrier_semaphore()
 
     def greet(j, _):
-        pl.semaphore_signal(
-            barrier, inc=1, device_id=place((me + j * step_by) % count), device_id_type=MESH
-        )
+        pl.semaphore_signal(barrier, inc=1, device_id=place(at_offset(j)), device_id_type=MESH)
         return 0
 
     lax.fori_loop(1, count, greet, 0, unroll=True)
@@ -106,13 +116,39 @@
         copy.start()
     voxel_copy = pltpu.make_async_copy(voxel_hbm, voxel, voxel_sem)
     voxel_copy.start()
+    own_feat = pltpu.make_async_copy(feats_hbm.at[:, columns(me)], got.at[0], feat_recv.at[0])
+    own_feat.start()
     halo[...] = jnp.zeros_like(halo)
     acc[...] = jnp.zeros_like(acc)
-    own_feat = pltpu.make_async_copy(
-        feats_hbm.at[:, pl.ds(pl.multiple_of(me * cols, cols), cols)], got.at[me], feat_recv.at[me]
-    )
-    own_extra = pltpu.make_async_copy(extra.at[me], got_extra.at[me], extra_recv.at[me])
-    own_feat.start()
+    gather[...] = jnp.zeros_like(gather)
+
+    def feat_copy(j):
+        to = at_offset(j)
+        return pltpu.make_async_remote_copy(
+            src_ref=feats_hbm.at[:, columns(to)],
+            dst_ref=got.at[j],
+            send_sem=feat_send.at[0],
+            recv_sem=feat_recv.at[j // group],
+            device_id=place(to),
+            device_id_type=MESH,
+        )
+
+    def extra_copy(j):
+        to = at_offset(j)
+        return pltpu.make_async_remote_copy(
+            src_ref=extra.at[to],
+            dst_ref=got_extra.at[j],
+            send_sem=extra_send.at[0],
+            recv_sem=extra_recv.at[j // group],
+            device_id=place(to),
+            device_id_type=MESH,
+        )
+
+    group = count // feat_recv.shape[0]
+    ahead = min(AHEAD, count)
+    pl.semaphore_wait(barrier, count - 1)
+    for j in range(1, ahead):
+        feat_copy(j).start()
 
     total_bricks = lists_ref.shape[1]
     groups = total_bricks // LANES
@@ -152,36 +188,17 @@
     for k in range(count):
         rows = slice(k * halves, (k + 1) * halves)
         extra[k] = jnp.concatenate([flat[rows, :], targets[rows]], axis=0).astype(jnp.bfloat16)
+    own_extra = pltpu.make_async_copy(extra.at[me], got_extra.at[0], extra_recv.at[0])
     own_extra.start()
-    pl.semaphore_wait(barrier, count - 1)
-
-    def feat_copy(to, frm):
-        return pltpu.make_async_remote_copy(
-            src_ref=feats_hbm.at[:, pl.ds(pl.multiple_of(to * cols, cols), cols)],
-            dst_ref=got.at[frm],
-            send_sem=feat_send.at[to],
-            recv_sem=feat_recv.at[frm],
-            device_id=place(to),
-            device_id_type=MESH,
-        )
-
-    def extra_copy(to, frm):
-        return pltpu.make_async_remote_copy(
-            src_ref=extra.at[to],
-            dst_ref=got_extra.at[frm],
-            send_sem=extra_send.at[to],
-            recv_sem=extra_recv.at[frm],
-            device_id=place(to),
-            device_id_type=MESH,
-        )
+    for j in range(1, ahead):
+        extra_copy(j).start()
 
     def send(j, _):
-        to = (me + j * step_by) % count
-        feat_copy(to, me).start()
-        extra_copy(to, me).start()
+        feat_copy(j).start()
+        extra_copy(j).start()
         return 0
 
-    lax.fori_loop(1, count, send, 0)
+    lax.fori_loop(ahead, count, send, 0, unroll=True)
     voxel_copy.wait()
     inputs[2].wait()
     inputs[3].wait()
@@ -201,58 +218,55 @@
         return 0
 
     lax.fori_loop(0, bricks // 4, squares, 0)
-    own_feat.wait()
-    own_extra.wait()
-
-    group = 4
-    while count % group:
-        group //= 2
-    lane = lax.broadcasted_iota(jnp.int32, (1, group * LANES), 1)
-    owner = (lane // slots) % per_half
+
+    span_all = group * LANES
+    owner = (lax.broadcasted_iota(jnp.int32, (1, span_all), 1) // slots) % per_half
+    across = [jnp.where(owner % side == j, 1.0, 0.0).astype(jnp.bfloat16) for j in range(side)]
+    along = owner // side == lax.broadcasted_iota(jnp.int32, (16, span_all), 0)
+
+    def arrived(ref, sems, g):
+        part_of = ref.at[pl.ds(g * group, group)]
+        return pltpu.make_async_remote_copy(
+            src_ref=part_of,
+            dst_ref=part_of,
+            send_sem=feat_send.at[0],
+            recv_sem=sems.at[g],
+            device_id=place(at_offset(1)),
+            device_id_type=MESH,
+        )
 
     def absorb(g, _):
-        sources = []
-        for u in range(group):
-            j = g * group + u
-            source = (me + (count - j) * step_by) % count
-            sources.append(source)
-            if u:
-                feat_copy(source, source).wait_recv()
-                extra_copy(source, source).wait_recv()
-            else:
-
-                @pl.when(g > 0)
-                def _():
-                    feat_copy(source, source).wait_recv()
-                    extra_copy(source, source).wait_recv()
-
+        arrived(got, feat_recv, g).wait_recv()
+        arrived(got_extra, extra_recv, g).wait_recv()
+        more = jnp.concatenate(
+            [got_extra[g * group + u].astype(jnp.float32) for u in range(group)], axis=1
+        )
         for h in range(halves):
             span = slice(h * LANES, (h + 1) * LANES)
-            x = jnp.concatenate([got[s, :, span] for s in sources], axis=1)
-            more = jnp.concatenate(
-                [got_extra[s].astype(jnp.float32) for s in sources], axis=1
-            )
-            live = more[h : h + 1]
-            target = more[halves + h : halves + h + 1].astype(jnp.bfloat16)
+            x = jnp.concatenate([got[g * group + u, :, span] for u in range(group)], axis=1)
+            live = jnp.where(along, more[h : h + 1], 0.0)
+            marked = live * more[halves + h : halves + h + 1]
             left = jnp.concatenate(
-                [x * jnp.where(owner == b, live, 0.0).astype(jnp.bfloat16) for b in range(per_half)],
+                [x * live[i : i + 1].astype(jnp.bfloat16) for i in range(tall)]
+                + [marked.astype(jnp.bfloat16)],
                 axis=0,
             )
-            right = jnp.concatenate(
-                [
-                    x,
-                    jnp.broadcast_to(target, (16, group * LANES)),
-                    jnp.zeros((LANES - feat - 16, group * LANES), jnp.bfloat16),
-                ],
-                axis=0,
-            )
-            rows = slice(h * per_half * feat, (h + 1) * per_half * feat)
-            acc[rows, :] += lax.dot_general(
+            right = jnp.concatenate([x * mask for mask in across], axis=0)
+            found = lax.dot_general(
                 left, right, (((1,), (1,)), ((), ())), preferred_element_type=jnp.float32
             )
+            acc[h * LANES : (h + 1) * LANES, :] += found[:LANES]
+            gather[h * tall : (h + 1) * tall, :] += found[LANES : LANES + tall]
         return 0
 
     lax.fori_loop(0, count // group, absorb, 0)
+
+    def unpack(ref, rows):
+        for e in range(side):
+            turned = rows if e == 0 else pltpu.roll(rows, LANES - e * feat, 1)
+            ref[pl.ds(e, bricks // side, stride=side), :] = turned
+
+    unpack(g_ref, gather[...])
 
     eye = lax.broadcasted_iota(jnp.int32, (1, feat, LANES), 1) == lax.broadcasted_iota(
         jnp.int32, (1, feat, LANES), 2
@@ -271,7 +285,22 @@
         return jnp.sum(jnp.where(eye, rows[:, None, :], 0.0), axis=2, keepdims=True)
 
     def gathered(t):
-        return block(acc, t)[:, :, feat : feat + 1]
+        return as_column(g_ref[at(t), :])
+
+    lane_block = lax.broadcasted_iota(jnp.int32, (1, 1, LANES), 2) // feat
+
+    def moments_times(step):
+        for t in range(chunks):
+            z_column = as_column(z_ref[step, at(t), :]).reshape(CHUNK // side, side, feat, 1)
+            spread_column = z_column[:, 0]
+            for e in range(1, side):
+                spread_column = jnp.where(lane_block == e, z_column[:, e], spread_column)
+            rows = CHUNK // side * feat
+            packed = acc[t * rows : (t + 1) * rows, :].reshape(CHUNK // side, feat, LANES)
+            mz_ref[t * (CHUNK // side) : (t + 1) * (CHUNK // side), :] = jnp.sum(
+                packed * spread_column, axis=1
+            )
+        unpack(my_ref, mz_ref[...])
 
     def begin(t, _):
         z_ref[0, at(t), :] = jnp.sum(block(square, t) * gathered(t), axis=1)
@@ -300,8 +329,8 @@
         return pltpu.make_async_remote_copy(
             src_ref=source,
             dst_ref=halo.at[step, k ^ 1],
-            send_sem=halo_send.at[step, k],
-            recv_sem=halo_recv.at[step, k ^ 1],
+            send_sem=halo_send.at[k],
+            recv_sem=halo_recv.at[step % 2, k ^ 1],
             device_id=beside[k],
             device_id_type=MESH,
         )
@@ -310,19 +339,30 @@
         return pltpu.make_async_remote_copy(
             src_ref=y_send.at[step, 0],
             dst_ref=halo.at[step, k],
-            send_sem=halo_send.at[step, k],
-            recv_sem=halo_recv.at[step, k],
+            send_sem=halo_send.at[k],
+            recv_sem=halo_recv.at[step % 2, k],
             device_id=beside[k],
             device_id_type=MESH,
         )
 
-    def part_copy(to, frm):
+    def part_copy(j):
         return pltpu.make_async_remote_copy(
             src_ref=part,
-            dst_ref=parts.at[frm],
-            send_sem=part_send.at[to],
-            recv_sem=part_recv.at[frm],
-            device_id=place(to),
+            dst_ref=parts.at[j],
+            send_sem=part_send.at[0],
+            recv_sem=part_recv.at[0],
+            device_id=place(at_offset(j)),
+            device_id_type=MESH,
+        )
+
+    def all_of(ref, send_sem, recv_sem):
+        whole = ref.at[pl.ds(1, count - 1)]
+        return pltpu.make_async_remote_copy(
+            src_ref=whole,
+            dst_ref=whole,
+            send_sem=send_sem.at[0],
+            recv_sem=recv_sem.at[0],
+            device_id=place(at_offset(1)),
             device_id_type=MESH,
         )
 
@@ -354,10 +394,10 @@
                 weighted = reg_ref[at(t), :] * made
                 column = jnp.sum(voxel[at(t)] * weighted[:, None, :], axis=2, keepdims=True)
                 q_ref[at(t), :] = jnp.sum(jnp.where(eye, column, 0.0), axis=1)
-            my_ref[at(t), :] = jnp.sum(block(acc, t) * as_column(z_ref[step, at(t), :]), axis=1)
             return 0
 
         lax.fori_loop(0, chunks, widen, 0)
+        moments_times(step)
         z = z_ref[step]
         ym_ref[1:bricks, :] = z[: bricks - 1]
         yp_ref[0 : bricks - 1, :] = z[1:]
@@ -371,6 +411,7 @@
             @pl.when(here[k])
             def _():
                 halo_arrived(step, k).wait_recv()
+                halo_copy(step, k).wait_send()
 
         xm = jnp.concatenate([halo[step, 0][8 - BY :], z[: bricks - BY]], axis=0)
         xp = jnp.concatenate([z[BY:], halo[step, 1][:BY]], axis=0)
@@ -408,10 +449,10 @@
     diagonal = entry == lax.broadcasted_iota(jnp.int32, (len(rows), LANES), 0)
     mine = jnp.sum(jnp.where(diagonal, sums, 0.0), axis=0, keepdims=True)
     part[...] = mine
-    parts[me] = mine
+    parts[0] = mine
 
     def start(j, _):
-        part_copy((me + j * step_by) % count, me).start()
+        part_copy(j).start()
         return 0
 
     lax.fori_loop(1, count, start, 0, unroll=True)
@@ -422,12 +463,10 @@
 
     lax.fori_loop(0, chunks, last, 0)
 
-    def finish(j, _):
-        source = (me + (count - j) * step_by) % count
-        part_copy(source, source).wait_recv()
-        return 0
-
-    lax.fori_loop(1, count, finish, 0)
+    all_of(got, feat_send, feat_recv).wait_send()
+    all_of(got_extra, extra_send, extra_recv).wait_send()
+    all_of(parts, part_send, part_recv).wait_send()
+    all_of(parts, part_send, part_recv).wait_recv()
     total = jnp.sum(parts[...], axis=0)
     spread_total = jnp.sum(
         jnp.where(diagonal, jnp.broadcast_to(total, diagonal.shape), 0.0), axis=1, keepdims=True
@@ -478,21 +517,6 @@
     image_ref[...] = combine(image)
     alpha_ref[...] = jnp.broadcast_to(alpha, alpha_ref.shape)
 
-    def drain(j, _):
-        to = (me + j * step_by) % count
-        feat_copy(to, me).wait_send()
-        extra_copy(to, me).wait_send()
-        part_copy(to, me).wait_send()
-        return 0
-
-    lax.fori_loop(1, count, drain, 0)
-    for step in range(ITERS):
-        for k in range(4):
-
-            @pl.when(here[k])
-            def _():
-                halo_copy(step, k).wait_send()
-
 
 def shards(gx, gy, point_feats, point_targets, point_lists, brick_adjacency, voxel_feats, voxel_reg):
     feat = point_feats.shape[0]
@@ -500,6 +524,9 @@
     bricks, _, vox = voxel_feats.shape
     count = gx * gy
     cols = bricks * slots
+    group = 4
+    while count % group:
+        group //= 2
     vmem = pl.BlockSpec(memory_space=pltpu.VMEM)
     hbm = pl.BlockSpec(memory_space=pltpu.HBM)
     f32 = jnp.float32
@@ -514,7 +541,10 @@
             pltpu.VMEM((count, 2 * cols // LANES, LANES), jnp.bfloat16),
             pltpu.VMEM((count * cols // LANES, LANES), f32),
             pltpu.VMEM((bricks, feat, vox), f32),
-            pltpu.VMEM((bricks * feat, LANES), f32),
+            pltpu.VMEM((bricks * feat * feat // LANES, LANES), f32),
+            pltpu.VMEM((bricks * feat // LANES, LANES), f32),
+            pltpu.VMEM((bricks * feat // LANES, LANES), f32),
+            pltpu.VMEM((bricks, LANES), f32),
             pltpu.VMEM((bricks * feat, LANES), f32),
             pltpu.VMEM((ITERS + 1, bricks, vox), f32),
             pltpu.VMEM((ITERS, bricks, LANES), f32),
@@ -533,14 +563,14 @@
             pltpu.VMEM((bricks, vox), f32),
             pltpu.SemaphoreType.DMA,
             pltpu.SemaphoreType.DMA((4,)),
-            pltpu.SemaphoreType.DMA((count,)),
-            pltpu.SemaphoreType.DMA((count,)),
-            pltpu.SemaphoreType.DMA((count,)),
-            pltpu.SemaphoreType.DMA((count,)),
-            pltpu.SemaphoreType.DMA((ITERS, 4)),
-            pltpu.SemaphoreType.DMA((ITERS, 4)),
-            pltpu.SemaphoreType.DMA((count,)),
-            pltpu.SemaphoreType.DMA((count,)),
+            pltpu.SemaphoreType.DMA((1,)),
+            pltpu.SemaphoreType.DMA((count // group,)),
+            pltpu.SemaphoreType.DMA((1,)),
+            pltpu.SemaphoreType.DMA((count // group,)),
+            pltpu.SemaphoreType.DMA((4,)),
+            pltpu.SemaphoreType.DMA((2, 4)),
+            pltpu.SemaphoreType.DMA((1,)),
+            pltpu.SemaphoreType.DMA((1,)),
         ],
         compiler_params=pltpu.CompilerParams(collective_id=0, has_side_effects=True, vmem_limit_bytes=16 * 1024 * 1024),
     )(

time: 40 us -> 37.4 us (0.935)
  Pallas kernels: 38.5 us -> 36 us
    pallas_call x1, Pallas kernels: 38.5 us -> 36 us  [shards(): pl.pallas_call(functools.partial(kernel, gx, gy), out_shape=(pltpu.VMEM((...]
where the time goes in v2:
time: 37.4 us; the launch traced here: 37.3 us
  Pallas kernels  36 us (96%)
  other arithmetic  0.67 us (2%)
  between operations  0.64 us (2%)
    pallas_call x1, Pallas kernels, shards(): pl.pallas_call(functools.partial(kernel, gx, gy), out_shape=(pltpu.VMEM((...  36 us

profile of v2, /device:TPU:0, one launch (start us, length us, event | category | flops | bytes accessed | tf_op | source)
XLA Modules:
  0.0 37.3 jit_solution(4528185803155885277)
XLA Ops:
  0.6 36.0 %shard_map.77 = (f32[32,512]{1,0:T(8,128)S(1)}, f32[32,512]{1,0:T(8,128)S(1)}, f32[32,512]{1,0:T(8,128)S(1)}, f32[32,512]{1,0:T(8,128)S(1)}, f32[1,512]{1,0:T(1,128)S(1)}) custom-call(bf16[32,8192]{1,0:T(8,128)(2,1)} %feats_hbm.1, bf16[64,128]{1,0:T(8,128)(2,1)} %bitcast.6, s32[8,1024]{1,0:T(8,128)} %bitcast.5, s32[4,32]{1,0:T(4,128)} %bitcast.7, ...), custom_call_target="tpu_custom_call" | custom-call | tf_op jit(solution)/shard_map/pallas_call | solution.py:533
  36.6 0.7 %multiply_subtract_fusion = (f32[32,512]{1,0:T(8,128)}, f32[32,512]{1,0:T(8,128)}) fusion(f32[32,512]{1,0:T(8,128)S(1)} %get-tuple-element.10, f32[32,512]{1,0:T(8,128)S(1)} %get-tuple-element.11, f32[512]{0:T(512)S(1)} %bitcast.4, f32[32,512]{1,0:T(8,128)S(1)} %get-tuple-element.7, f32[32,512]{1,0:T(8,128)S(1)} %get-tuple-element.9), kind=kLoop, calls=%fused_computation | loop fusion | flops 65536 | bytes 395264 | tf_op jit(solution)/shard_map/sub | solution.py:589

commit v3 on v2

--- a/solution.py
+++ b/solution.py
@@ -16,7 +16,6 @@
 MESH = pl.DeviceIdType.MESH
 STRIDE = 11
 SCALE = 2.0**-8
-AHEAD = 8
 SHIFTS = (8.0, 1.0, 4.0)
 
 coupling_weight = 1.0
@@ -39,6 +38,8 @@
     got,
     got_extra,
     extra,
+    acc_far,
+    gather_far,
     flat,
     voxel,
     acc,
@@ -67,6 +68,8 @@
     feat_recv,
     extra_send,
     extra_recv,
+    far_send,
+    far_recv,
     halo_send,
     halo_recv,
     part_send,
@@ -75,15 +78,21 @@
     count = gx * gy
     ix, iy = lax.axis_index("gx"), lax.axis_index("gy")
     me = ix * gy + iy
-    feat, cols = got.shape[1], got.shape[2]
+    feat = got.shape[2]
+    total_bricks, slots = lists_ref.shape[1], lists_ref.shape[0]
+    near = got.shape[1]
+    wings = count // near
+    first = me // near * near
+    group = near // feat_recv.shape[1]
     bricks = reg_ref.shape[0]
-    slots = cols // bricks
+    cols = bricks * slots
     halves = cols // LANES
     per_half = LANES // slots
     side = LANES // feat
     tall = per_half // side
 
     step_by = STRIDE if math.gcd(STRIDE, count) == 1 else 1
+    kinds = [(w, h) for w in reversed(range(wings)) for h in range(halves)]
 
     def place(index):
         return (index // gy, index % gy)
@@ -91,8 +100,12 @@
     def at_offset(j):
         return (me + j * step_by) % count
 
-    def columns(index):
-        return pl.ds(pl.multiple_of(index * cols, cols), cols)
+    def near_offset(j):
+        return first + (me - first + j * step_by) % near
+
+    def columns(index, w, h):
+        start = (index + w * near) % count * cols + h * LANES
+        return pl.ds(pl.multiple_of(start, LANES), LANES)
 
     barrier = pltpu.get_barrier_semaphore()
 
@@ -116,41 +129,36 @@
         copy.start()
     voxel_copy = pltpu.make_async_copy(voxel_hbm, voxel, voxel_sem)
     voxel_copy.start()
-    own_feat = pltpu.make_async_copy(feats_hbm.at[:, columns(me)], got.at[0], feat_recv.at[0])
-    own_feat.start()
+    for q, (w, h) in enumerate(kinds):
+        pltpu.make_async_copy(
+            feats_hbm.at[:, columns(me, w, h)], got.at[q, 0], feat_recv.at[q, 0]
+        ).start()
     halo[...] = jnp.zeros_like(halo)
     acc[...] = jnp.zeros_like(acc)
     gather[...] = jnp.zeros_like(gather)
 
-    def feat_copy(j):
-        to = at_offset(j)
+    def feat_copy(q, j):
+        to = near_offset(j)
         return pltpu.make_async_remote_copy(
-            src_ref=feats_hbm.at[:, columns(to)],
-            dst_ref=got.at[j],
+            src_ref=feats_hbm.at[:, columns(to, *kinds[q])],
+            dst_ref=got.at[q, j],
             send_sem=feat_send.at[0],
-            recv_sem=feat_recv.at[j // group],
+            recv_sem=feat_recv.at[q, j // group],
             device_id=place(to),
             device_id_type=MESH,
         )
 
     def extra_copy(j):
-        to = at_offset(j)
+        to = near_offset(j)
         return pltpu.make_async_remote_copy(
-            src_ref=extra.at[to],
+            src_ref=extra.at[to % near],
             dst_ref=got_extra.at[j],
             send_sem=extra_send.at[0],
-            recv_sem=extra_recv.at[j // group],
+            recv_sem=extra_recv.at[0],
             device_id=place(to),
             device_id_type=MESH,
         )
 
-    group = count // feat_recv.shape[0]
-    ahead = min(AHEAD, count)
-    pl.semaphore_wait(barrier, count - 1)
-    for j in range(1, ahead):
-        feat_copy(j).start()
-
-    total_bricks = lists_ref.shape[1]
     groups = total_bricks // LANES
     wide = slots * LANES
     inputs[0].wait()
@@ -187,18 +195,28 @@
     targets = target_ref[...].astype(jnp.float32)
     for k in range(count):
         rows = slice(k * halves, (k + 1) * halves)
-        extra[k] = jnp.concatenate([flat[rows, :], targets[rows]], axis=0).astype(jnp.bfloat16)
-    own_extra = pltpu.make_async_copy(extra.at[me], got_extra.at[0], extra_recv.at[0])
-    own_extra.start()
-    for j in range(1, ahead):
-        extra_copy(j).start()
-
-    def send(j, _):
-        feat_copy(j).start()
+        wing = (k // near + count - me // near) % wings if wings > 1 else 0
+        extra[k % near, wing] = jnp.concatenate([flat[rows, :], targets[rows]], axis=0).astype(
+            jnp.bfloat16
+        )
+    pltpu.make_async_copy(extra.at[me % near], got_extra.at[0], extra_recv.at[0]).start()
+
+    pl.semaphore_wait(barrier, count - 1)
+
+    def send_feats(q):
+        def send(j, _):
+            feat_copy(q, j).start()
+            return 0
+
+        lax.fori_loop(1, near, send, 0, unroll=True)
+
+    def send_extra(j, _):
         extra_copy(j).start()
         return 0
 
-    lax.fori_loop(ahead, count, send, 0, unroll=True)
+    lax.fori_loop(1, near, send_extra, 0, unroll=True)
+    for q in range(len(kinds)):
+        send_feats(q)
     voxel_copy.wait()
     inputs[2].wait()
     inputs[3].wait()
@@ -224,26 +242,26 @@
     across = [jnp.where(owner % side == j, 1.0, 0.0).astype(jnp.bfloat16) for j in range(side)]
     along = owner // side == lax.broadcasted_iota(jnp.int32, (16, span_all), 0)
 
-    def arrived(ref, sems, g):
-        part_of = ref.at[pl.ds(g * group, group)]
+    def arrived(ref, sem):
         return pltpu.make_async_remote_copy(
-            src_ref=part_of,
-            dst_ref=part_of,
+            src_ref=ref,
+            dst_ref=ref,
             send_sem=feat_send.at[0],
-            recv_sem=sems.at[g],
+            recv_sem=sem,
             device_id=place(at_offset(1)),
             device_id_type=MESH,
         )
 
-    def absorb(g, _):
-        arrived(got, feat_recv, g).wait_recv()
-        arrived(got_extra, extra_recv, g).wait_recv()
-        more = jnp.concatenate(
-            [got_extra[g * group + u].astype(jnp.float32) for u in range(group)], axis=1
-        )
-        for h in range(halves):
-            span = slice(h * LANES, (h + 1) * LANES)
-            x = jnp.concatenate([got[g * group + u, :, span] for u in range(group)], axis=1)
+    def absorb(q):
+        w, h = kinds[q]
+
+        def some(g, _):
+            mine = pl.ds(g * group, group)
+            arrived(got.at[q, mine], feat_recv.at[q, g]).wait_recv()
+            x = jnp.concatenate([got[q, g * group + u] for u in range(group)], axis=1)
+            more = jnp.concatenate(
+                [got_extra[g * group + u, w].astype(jnp.float32) for u in range(group)], axis=1
+            )
             live = jnp.where(along, more[h : h + 1], 0.0)
             marked = live * more[halves + h : halves + h + 1]
             left = jnp.concatenate(
@@ -255,18 +273,50 @@
             found = lax.dot_general(
                 left, right, (((1,), (1,)), ((), ())), preferred_element_type=jnp.float32
             )
-            acc[h * LANES : (h + 1) * LANES, :] += found[:LANES]
-            gather[h * tall : (h + 1) * tall, :] += found[LANES : LANES + tall]
-        return 0
-
-    lax.fori_loop(0, count // group, absorb, 0)
+            acc[w, h * LANES : (h + 1) * LANES, :] += found[:LANES]
+            gather[w, h * tall : (h + 1) * tall, :] += found[LANES : LANES + tall]
+            return 0
+
+        lax.fori_loop(0, near // group, some, 0)
+
+    def far_copy(source, target, e):
+        return pltpu.make_async_remote_copy(
+            src_ref=source,
+            dst_ref=target,
+            send_sem=far_send.at[e],
+            recv_sem=far_recv.at[e],
+            device_id=place((me + near) % count),
+            device_id_type=MESH,
+        )
+
+    def far_moments(piece):
+        rows = pl.ds(piece * LANES // 2, LANES // 2)
+        return far_copy(acc.at[1, rows], acc_far.at[rows], 0)
+
+    far_gather = far_copy(gather.at[1], gather_far, 1)
+    all_far_moments = far_copy(acc.at[1], acc_far, 0)
+
+    arrived(got_extra, extra_recv.at[0]).wait_recv()
+    for q, (w, h) in enumerate(kinds):
+        absorb(q)
+        if w:
+            pieces_done = 2 * h + 1
+            if h + 1 == halves:
+                far_gather.start()
+                pieces_done = 2 * halves
+            for piece in range(max(2 * h - 1, 0), pieces_done):
+                far_moments(piece).start()
 
     def unpack(ref, rows):
         for e in range(side):
             turned = rows if e == 0 else pltpu.roll(rows, LANES - e * feat, 1)
             ref[pl.ds(e, bricks // side, stride=side), :] = turned
 
-    unpack(g_ref, gather[...])
+    found_gather = gather[0]
+    if wings > 1:
+        far_gather.wait_recv()
+        found_gather = found_gather + gather_far[...]
+    unpack(g_ref, found_gather)
 
     eye = lax.broadcasted_iota(jnp.int32, (1, feat, LANES), 1) == lax.broadcasted_iota(
         jnp.int32, (1, feat, LANES), 2
@@ -296,7 +346,7 @@
             for e in range(1, side):
                 spread_column = jnp.where(lane_block == e, z_column[:, e], spread_column)
             rows = CHUNK // side * feat
-            packed = acc[t * rows : (t + 1) * rows, :].reshape(CHUNK // side, feat, LANES)
+            packed = acc[0, t * rows : (t + 1) * rows, :].reshape(CHUNK // side, feat, LANES)
             mz_ref[t * (CHUNK // side) : (t + 1) * (CHUNK // side), :] = jnp.sum(
                 packed * spread_column, axis=1
             )
@@ -355,16 +405,15 @@
             device_id_type=MESH,
         )
 
-    def all_of(ref, send_sem, recv_sem):
-        whole = ref.at[pl.ds(1, count - 1)]
-        return pltpu.make_async_remote_copy(
-            src_ref=whole,
-            dst_ref=whole,
-            send_sem=send_sem.at[0],
-            recv_sem=recv_sem.at[0],
+    def sent(ref, sem):
+        pltpu.make_async_remote_copy(
+            src_ref=ref,
+            dst_ref=ref,
+            send_sem=sem,
+            recv_sem=part_recv.at[0],
             device_id=place(at_offset(1)),
             device_id_type=MESH,
-        )
+        ).wait_send()
 
     def fold(values):
         total = jnp.sum(values, axis=0, keepdims=True)
@@ -397,6 +446,9 @@
             return 0
 
         lax.fori_loop(0, chunks, widen, 0)
+        if step == 0 and wings > 1:
+            all_far_moments.wait_recv()
+            acc[0] += acc_far[...]
         moments_times(step)
         z = z_ref[step]
         ym_ref[1:bricks, :] = z[: bricks - 1]
@@ -463,10 +515,14 @@
 
     lax.fori_loop(0, chunks, last, 0)
 
-    all_of(got, feat_send, feat_recv).wait_send()
-    all_of(got_extra, extra_send, extra_recv).wait_send()
-    all_of(parts, part_send, part_recv).wait_send()
-    all_of(parts, part_send, part_recv).wait_recv()
+    sent(got.at[:, pl.ds(1, near - 1)], feat_send.at[0])
+    sent(got_extra.at[pl.ds(1, near - 1)], extra_send.at[0])
+    if wings > 1:
+        far_gather.wait_send()
+        all_far_moments.wait_send()
+    others = parts.at[pl.ds(1, count - 1)]
+    sent(others, part_send.at[0])
+    arrived(others, part_recv.at[0]).wait_recv()
     total = jnp.sum(parts[...], axis=0)
     spread_total = jnp.sum(
         jnp.where(diagonal, jnp.broadcast_to(total, diagonal.shape), 0.0), axis=1, keepdims=True
@@ -524,8 +580,10 @@
     bricks, _, vox = voxel_feats.shape
     count = gx * gy
     cols = bricks * slots
-    group = 4
-    while count % group:
+    wings = 2 if gx % 2 == 0 else 1
+    near = count // wings
+    group = 8
+    while near % group:
         group //= 2
     vmem = pl.BlockSpec(memory_space=pltpu.VMEM)
     hbm = pl.BlockSpec(memory_space=pltpu.HBM)
@@ -536,13 +594,15 @@
         in_specs=[hbm] * 6,
         out_specs=(vmem,) * 5,
         scratch_shapes=[
-            pltpu.VMEM((count, feat, cols), jnp.bfloat16),
-            pltpu.VMEM((count, 2 * cols // LANES, LANES), jnp.bfloat16),
-            pltpu.VMEM((count, 2 * cols // LANES, LANES), jnp.bfloat16),
+            pltpu.VMEM((wings * cols // LANES, near, feat, LANES), jnp.bfloat16),
+            pltpu.VMEM((near, wings, 2 * cols // LANES, LANES), jnp.bfloat16),
+            pltpu.VMEM((near, wings, 2 * cols // LANES, LANES), jnp.bfloat16),
+            pltpu.VMEM((bricks * feat * feat // LANES, LANES), f32),
+            pltpu.VMEM((bricks * feat // LANES, LANES), f32),
             pltpu.VMEM((count * cols // LANES, LANES), f32),
             pltpu.VMEM((bricks, feat, vox), f32),
-            pltpu.VMEM((bricks * feat * feat // LANES, LANES), f32),
-            pltpu.VMEM((bricks * feat // LANES, LANES), f32),
+            pltpu.VMEM((wings, bricks * feat * feat // LANES, LANES), f32),
+            pltpu.VMEM((wings, bricks * feat // LANES, LANES), f32),
             pltpu.VMEM((bricks * feat // LANES, LANES), f32),
             pltpu.VMEM((bricks, LANES), f32),
             pltpu.VMEM((bricks * feat, LANES), f32),
@@ -564,9 +624,11 @@
             pltpu.SemaphoreType.DMA,
             pltpu.SemaphoreType.DMA((4,)),
             pltpu.SemaphoreType.DMA((1,)),
-            pltpu.SemaphoreType.DMA((count // group,)),
+            pltpu.SemaphoreType.DMA((wings * cols // LANES, near // group)),
             pltpu.SemaphoreType.DMA((1,)),
-            pltpu.SemaphoreType.DMA((count // group,)),
+            pltpu.SemaphoreType.DMA((1,)),
+            pltpu.SemaphoreType.DMA((2,)),
+            pltpu.SemaphoreType.DMA((2,)),
             pltpu.SemaphoreType.DMA((4,)),
             pltpu.SemaphoreType.DMA((2, 4)),
             pltpu.SemaphoreType.DMA((1,)),

time: 37.4 us -> 34.9 us (0.933)
  Pallas kernels: 36 us -> 33.4 us
    pallas_call x1, Pallas kernels: 36 us -> 33.4 us  [shards(): pl.pallas_call(functools.partial(kernel, gx, gy), out_shape=(pltpu.VMEM((...]
where the time goes in v3:
time: 34.9 us; the launch traced here: 34.7 us
  Pallas kernels  33.4 us (96%)
  other arithmetic  0.67 us (2%)
  between operations  0.64 us (2%)
    pallas_call x1, Pallas kernels, shards(): pl.pallas_call(functools.partial(kernel, gx, gy), out_shape=(pltpu.VMEM((...  33.4 us

profile of v3, /device:TPU:0, one launch (start us, length us, event | category | flops | bytes accessed | tf_op | source)
XLA Modules:
  0.0 34.7 jit_solution(5929672036412076050)
XLA Ops:
  0.6 33.4 %shard_map.77 = (f32[32,512]{1,0:T(8,128)S(1)}, f32[32,512]{1,0:T(8,128)S(1)}, f32[32,512]{1,0:T(8,128)S(1)}, f32[32,512]{1,0:T(8,128)S(1)}, f32[1,512]{1,0:T(1,128)S(1)}) custom-call(bf16[32,8192]{1,0:T(8,128)(2,1)} %feats_hbm.1, bf16[64,128]{1,0:T(8,128)(2,1)} %bitcast.6, s32[8,1024]{1,0:T(8,128)} %bitcast.5, s32[4,32]{1,0:T(4,128)} %bitcast.7, ...), custom_call_target="tpu_custom_call" | custom-call | tf_op jit(solution)/shard_map/pallas_call | solution.py:591
  34.1 0.7 %multiply_subtract_fusion = (f32[32,512]{1,0:T(8,128)}, f32[32,512]{1,0:T(8,128)}) fusion(f32[32,512]{1,0:T(8,128)S(1)} %get-tuple-element.10, f32[32,512]{1,0:T(8,128)S(1)} %get-tuple-element.11, f32[512]{0:T(512)S(1)} %bitcast.4, f32[32,512]{1,0:T(8,128)S(1)} %get-tuple-element.7, f32[32,512]{1,0:T(8,128)S(1)} %get-tuple-element.9), kind=kLoop, calls=%fused_computation | loop fusion | flops 65536 | bytes 395264 | tf_op jit(solution)/shard_map/sub | solution.py:651

commit v4 on v3

--- a/solution.py
+++ b/solution.py
@@ -12,6 +12,7 @@
 BY = 4
 ITERS = 3
 LANES = 128
+SUBLANES = 8
 CHUNK = 8
 MESH = pl.DeviceIdType.MESH
 STRIDE = 11
@@ -38,6 +39,7 @@
     got,
     got_extra,
     extra,
+    acc_sent,
     acc_far,
     gather_far,
     flat,
@@ -74,6 +76,7 @@
     halo_recv,
     part_send,
     part_recv,
+    ready,
 ):
     count = gx * gy
     ix, iy = lax.axis_index("gx"), lax.axis_index("gy")
@@ -109,11 +112,17 @@
 
     barrier = pltpu.get_barrier_semaphore()
 
+    partner = place((me + near) % count)
+    wing = me // near
+    first_wing = wing == 0
+    last_wing = wing == wings - 1
+
     def greet(j, _):
-        pl.semaphore_signal(barrier, inc=1, device_id=place(at_offset(j)), device_id_type=MESH)
+        pl.semaphore_signal(
+            barrier, inc=1, device_id=place(near_offset(j)), device_id_type=MESH
+        )
         return 0
 
-    lax.fori_loop(1, count, greet, 0, unroll=True)
     inputs = [
         pltpu.make_async_copy(source, target, input_sem.at[e])
         for e, (source, target) in enumerate(
@@ -125,8 +134,17 @@
             ]
         )
     ]
-    for copy in inputs:
-        copy.start()
+    inputs[0].start()
+    inputs[1].start()
+    lax.fori_loop(1, near, greet, 0, unroll=True)
+    if wings > 1:
+
+        @pl.when(first_wing)
+        def _():
+            pl.semaphore_signal(barrier, inc=1, device_id=partner, device_id_type=MESH)
+
+    inputs[2].start()
+    inputs[3].start()
     voxel_copy = pltpu.make_async_copy(voxel_hbm, voxel, voxel_sem)
     voxel_copy.start()
     for q, (w, h) in enumerate(kinds):
@@ -195,13 +213,19 @@
     targets = target_ref[...].astype(jnp.float32)
     for k in range(count):
         rows = slice(k * halves, (k + 1) * halves)
-        wing = (k // near + count - me // near) % wings if wings > 1 else 0
-        extra[k % near, wing] = jnp.concatenate([flat[rows, :], targets[rows]], axis=0).astype(
+        from_me = (k // near + wings - wing) % wings if wings > 1 else 0
+        extra[k % near, from_me] = jnp.concatenate([flat[rows, :], targets[rows]], axis=0).astype(
             jnp.bfloat16
         )
     pltpu.make_async_copy(extra.at[me % near], got_extra.at[0], extra_recv.at[0]).start()
 
-    pl.semaphore_wait(barrier, count - 1)
+    pl.semaphore_wait(barrier, near - 1 + wing)
+    if wings > 1:
+
+        @pl.when(last_wing)
+        def _():
+            pl.semaphore_signal(ready, inc=1, device_id=partner, device_id_type=MESH)
+
 
     def send_feats(q):
         def send(j, _):
@@ -236,6 +260,16 @@
         return 0
 
     lax.fori_loop(0, bricks // 4, squares, 0)
+    linked = jnp.where(adjacency_ref[...] >= 0, 1.0, 0.0)
+    same_brick = lax.broadcasted_iota(jnp.int32, (bricks, bricks), 0) == lax.broadcasted_iota(
+        jnp.int32, (bricks, bricks), 1
+    )
+    weights = [
+        jnp.sum(jnp.where(same_brick, linked[k : k + 1], 0.0), axis=1, keepdims=True)
+        for k in range(4)
+    ]
+    masks = [w > 0.0 for w in weights]
+    degree = weights[0] + weights[1] + weights[2] + weights[3]
 
     span_all = group * LANES
     owner = (lax.broadcasted_iota(jnp.int32, (1, span_all), 1) // slots) % per_half
@@ -285,27 +319,91 @@
             dst_ref=target,
             send_sem=far_send.at[e],
             recv_sem=far_recv.at[e],
-            device_id=place((me + near) % count),
+            device_id=partner,
             device_id_type=MESH,
         )
 
-    def far_moments(piece):
-        rows = pl.ds(piece * LANES // 2, LANES // 2)
-        return far_copy(acc.at[1, rows], acc_far.at[rows], 0)
+    tiles = feat // SUBLANES
+    middle = tiles // 2
+    in_block = lax.broadcasted_iota(jnp.int32, (SUBLANES, LANES), 1) % feat
+    lane_block = lax.broadcasted_iota(jnp.int32, (1, LANES), 1) // feat
+
+    def pack(h):
+        found = []
+        for i in range(0, tall, 2):
+            rows = [
+                [
+                    acc[1, pl.ds(h * LANES + (i + k) * feat + r * SUBLANES, SUBLANES), :]
+                    for r in range(tiles)
+                ]
+                for k in range(2)
+            ]
+            found = found + [rows[0][0], rows[1][0]]
+            for k in range(2):
+                for r in range(1, middle):
+                    turned = pltpu.roll(rows[k][tiles - r], r * SUBLANES, 1)
+                    found.append(jnp.where(in_block >= r * SUBLANES, rows[k][r], turned))
+            turned = pltpu.roll(rows[1][middle], middle * SUBLANES, 1)
+            found.append(jnp.where(in_block >= middle * SUBLANES, rows[0][middle], turned))
+        packed = jnp.concatenate(found, axis=0)
+        acc_sent[h * packed.shape[0] : (h + 1) * packed.shape[0], :] = packed
+
+    def unpack_far(h):
+        upper, above = [], []
+        each = tiles + 1
+        for i in range(0, tall, 2):
+            start = (h * tall // 2 + i // 2) * each
+            given = [
+                acc_far[pl.ds((start + r) * SUBLANES, SUBLANES), :] for r in range(each)
+            ]
+            for k in range(2):
+                rows = [given[k]] + [None] * (tiles - 1)
+                for r in range(1, middle):
+                    both = given[2 + k * (middle - 1) + r - 1]
+                    rows[r] = both
+                    rows[tiles - r] = pltpu.roll(both, LANES - r * SUBLANES, 1)
+                last_tile = given[each - 1]
+                rows[middle] = (
+                    pltpu.roll(last_tile, LANES - middle * SUBLANES, 1) if k else last_tile
+                )
+                for r in range(tiles):
+                    upper.append(jnp.where(in_block >= r * SUBLANES, rows[r], 0.0))
+                    above.append(jnp.where(in_block >= (r + 1) * SUBLANES, rows[r], 0.0))
+        turned = jnp.concatenate(above, axis=0).T
+        below = []
+        for i in range(tall):
+            mine = jnp.zeros((feat, LANES), jnp.float32)
+            for j in range(side):
+                band = turned[j * feat : (j + 1) * feat]
+                if i != j:
+                    band = pltpu.roll(band, (j - i) % side * feat, 1)
+                mine = jnp.where(lane_block == j, band, mine)
+            below.append(mine)
+        rows = slice(h * LANES, (h + 1) * LANES)
+        acc[0, rows, :] += jnp.concatenate(upper, axis=0) + jnp.concatenate(below, axis=0)
+
+    def far_moments(h):
+        half = acc_sent.shape[0] // halves
+        rows = pl.ds(h * half, half)
+        return far_copy(acc_sent.at[rows], acc_far.at[rows], 0)
 
     far_gather = far_copy(gather.at[1], gather_far, 1)
-    all_far_moments = far_copy(acc.at[1], acc_far, 0)
+    all_far_moments = far_copy(acc_sent, acc_far, 0)
 
     arrived(got_extra, extra_recv.at[0]).wait_recv()
     for q, (w, h) in enumerate(kinds):
         absorb(q)
         if w:
-            pieces_done = 2 * h + 1
+            pack(h)
+            if h == 0:
+
+                @pl.when(first_wing)
+                def _():
+                    pl.semaphore_wait(ready, 1)
+
             if h + 1 == halves:
                 far_gather.start()
-                pieces_done = 2 * halves
-            for piece in range(max(2 * h - 1, 0), pieces_done):
-                far_moments(piece).start()
+            far_moments(h).start()
 
     def unpack(ref, rows):
         for e in range(side):
@@ -336,8 +434,6 @@
 
     def gathered(t):
         return as_column(g_ref[at(t), :])
-
-    lane_block = lax.broadcasted_iota(jnp.int32, (1, 1, LANES), 2) // feat
 
     def moments_times(step):
         for t in range(chunks):
@@ -358,16 +454,6 @@
 
     lax.fori_loop(0, chunks, begin, 0, unroll=True)
 
-    linked = jnp.where(adjacency_ref[...] >= 0, 1.0, 0.0)
-    same_brick = lax.broadcasted_iota(jnp.int32, (bricks, bricks), 0) == lax.broadcasted_iota(
-        jnp.int32, (bricks, bricks), 1
-    )
-    weights = [
-        jnp.sum(jnp.where(same_brick, linked[k : k + 1], 0.0), axis=1, keepdims=True)
-        for k in range(4)
-    ]
-    masks = [w > 0.0 for w in weights]
-    degree = weights[0] + weights[1] + weights[2] + weights[3]
     here = [ix > 0, ix < gx - 1, iy > 0, iy < gy - 1]
     beside = [(ix - 1, iy), (ix + 1, iy), (ix, iy - 1), (ix, iy + 1)]
 
@@ -448,7 +534,8 @@
         lax.fori_loop(0, chunks, widen, 0)
         if step == 0 and wings > 1:
             all_far_moments.wait_recv()
-            acc[0] += acc_far[...]
+            for h in range(halves):
+                unpack_far(h)
         moments_times(step)
         z = z_ref[step]
         ym_ref[1:bricks, :] = z[: bricks - 1]
@@ -581,6 +668,7 @@
     count = gx * gy
     cols = bricks * slots
     wings = 2 if gx % 2 == 0 else 1
+    kept = bricks * feat * (feat + SUBLANES) // 2 // LANES
     near = count // wings
     group = 8
     while near % group:
@@ -597,7 +685,8 @@
             pltpu.VMEM((wings * cols // LANES, near, feat, LANES), jnp.bfloat16),
             pltpu.VMEM((near, wings, 2 * cols // LANES, LANES), jnp.bfloat16),
             pltpu.VMEM((near, wings, 2 * cols // LANES, LANES), jnp.bfloat16),
-            pltpu.VMEM((bricks * feat * feat // LANES, LANES), f32),
+            pltpu.VMEM((kept, LANES), f32),
+            pltpu.VMEM((kept, LANES), f32),
             pltpu.VMEM((bricks * feat // LANES, LANES), f32),
             pltpu.VMEM((count * cols // LANES, LANES), f32),
             pltpu.VMEM((bricks, feat, vox), f32),
@@ -633,6 +722,7 @@
             pltpu.SemaphoreType.DMA((2, 4)),
             pltpu.SemaphoreType.DMA((1,)),
             pltpu.SemaphoreType.DMA((1,)),
+            pltpu.SemaphoreType.REGULAR,
         ],
         compiler_params=pltpu.CompilerParams(collective_id=0, has_side_effects=True, vmem_limit_bytes=16 * 1024 * 1024),
     )(

time: 34.9 us -> 32.7 us (0.937)
  Pallas kernels: 33.4 us -> 31.2 us
    pallas_call x1, Pallas kernels: 33.4 us -> 31.2 us  [shards(): pl.pallas_call(functools.partial(kernel, gx, gy), out_shape=(pltpu.VMEM((...]
where the time goes in v4:
time: 32.7 us; the launch traced here: 32.5 us
  Pallas kernels  31.2 us (95%)
  other arithmetic  0.67 us (2%)
  between operations  0.64 us (2%)
    pallas_call x1, Pallas kernels, shards(): pl.pallas_call(functools.partial(kernel, gx, gy), out_shape=(pltpu.VMEM((...  31.2 us
    sub x1, other arithmetic, shards(): return (answer + alpha * direction, res - alpha * image)  0.67 us

profile of v4, /device:TPU:0, one launch (start us, length us, event | category | flops | bytes accessed | tf_op | source)
XLA Modules:
  0.0 32.5 jit_solution(11121046566980973673)
XLA Ops:
  0.6 31.2 %shard_map.77 = (f32[32,512]{1,0:T(8,128)S(1)}, f32[32,512]{1,0:T(8,128)S(1)}, f32[32,512]{1,0:T(8,128)S(1)}, f32[32,512]{1,0:T(8,128)S(1)}, f32[1,512]{1,0:T(1,128)S(1)}) custom-call(bf16[32,8192]{1,0:T(8,128)(2,1)} %feats_hbm.1, bf16[64,128]{1,0:T(8,128)(2,1)} %bitcast.6, s32[8,1024]{1,0:T(8,128)} %bitcast.5, s32[4,32]{1,0:T(4,128)} %bitcast.7, ...), custom_call_target="tpu_custom_call" | custom-call | tf_op jit(solution)/shard_map/pallas_call | solution.py:679
  31.9 0.7 %multiply_subtract_fusion = (f32[32,512]{1,0:T(8,128)}, f32[32,512]{1,0:T(8,128)}) fusion(f32[32,512]{1,0:T(8,128)S(1)} %get-tuple-element.10, f32[32,512]{1,0:T(8,128)S(1)} %get-tuple-element.11, f32[512]{0:T(512)S(1)} %bitcast.4, f32[32,512]{1,0:T(8,128)S(1)} %get-tuple-element.7, f32[32,512]{1,0:T(8,128)S(1)} %get-tuple-element.9), kind=kLoop, calls=%fused_computation | loop fusion | flops 65536 | bytes 395264 | tf_op jit(solution)/shard_map/sub | solution.py:741

commit v5 on v4

--- a/solution.py
+++ b/solution.py
@@ -17,6 +17,7 @@
 MESH = pl.DeviceIdType.MESH
 STRIDE = 11
 SCALE = 2.0**-8
+UNUSED = 256.0
 SHIFTS = (8.0, 1.0, 4.0)
 
 coupling_weight = 1.0
@@ -94,34 +95,37 @@
     side = LANES // feat
     tall = per_half // side
 
-    step_by = STRIDE if math.gcd(STRIDE, count) == 1 else 1
+    half_gx = gx // wings
+    first_x = ix // half_gx * half_gx
+    rows_at = [(ix - first_x + a) % half_gx for a in range(half_gx)]
+    across_at = [(iy + b) % gy for b in range(gy)]
+    all_rows_at = [(ix + a) % gx for a in range(gx)]
+    step_by = STRIDE if math.gcd(STRIDE, near) == 1 else 1
+    offsets = [divmod(j * step_by % near, gy) for j in range(near)]
+    part_order = list(range(count - 1, 0, -1))
     kinds = [(w, h) for w in reversed(range(wings)) for h in range(halves)]
 
-    def place(index):
-        return (index // gy, index % gy)
-
-    def at_offset(j):
-        return (me + j * step_by) % count
-
-    def near_offset(j):
-        return first + (me - first + j * step_by) % near
-
-    def columns(index, w, h):
-        start = (index + w * near) % count * cols + h * LANES
+    def near_index(j):
+        a, b = offsets[j]
+        return rows_at[a] * gy + across_at[b]
+
+    def near_place(j):
+        a, b = offsets[j]
+        return (first_x + rows_at[a], across_at[b])
+
+    def columns(j, w, h):
+        start = ((first_x + w * half_gx) % gx * gy + near_index(j)) * cols + h * LANES
         return pl.ds(pl.multiple_of(start, LANES), LANES)
 
     barrier = pltpu.get_barrier_semaphore()
 
-    partner = place((me + near) % count)
+    partner = ((ix + half_gx) % gx, iy)
     wing = me // near
     first_wing = wing == 0
     last_wing = wing == wings - 1
 
-    def greet(j, _):
-        pl.semaphore_signal(
-            barrier, inc=1, device_id=place(near_offset(j)), device_id_type=MESH
-        )
-        return 0
+    def greet(j):
+        pl.semaphore_signal(barrier, inc=1, device_id=near_place(j), device_id_type=MESH)
 
     inputs = [
         pltpu.make_async_copy(source, target, input_sem.at[e])
@@ -136,7 +140,8 @@
     ]
     inputs[0].start()
     inputs[1].start()
-    lax.fori_loop(1, near, greet, 0, unroll=True)
+    for j in range(1, near):
+        greet(j)
     if wings > 1:
 
         @pl.when(first_wing)
@@ -149,31 +154,29 @@
     voxel_copy.start()
     for q, (w, h) in enumerate(kinds):
         pltpu.make_async_copy(
-            feats_hbm.at[:, columns(me, w, h)], got.at[q, 0], feat_recv.at[q, 0]
+            feats_hbm.at[:, columns(0, w, h)], got.at[q, 0], feat_recv.at[q, 0]
         ).start()
     halo[...] = jnp.zeros_like(halo)
     acc[...] = jnp.zeros_like(acc)
     gather[...] = jnp.zeros_like(gather)
 
     def feat_copy(q, j):
-        to = near_offset(j)
         return pltpu.make_async_remote_copy(
-            src_ref=feats_hbm.at[:, columns(to, *kinds[q])],
+            src_ref=feats_hbm.at[:, columns(j, *kinds[q])],
             dst_ref=got.at[q, j],
             send_sem=feat_send.at[0],
             recv_sem=feat_recv.at[q, j // group],
-            device_id=place(to),
+            device_id=near_place(j),
             device_id_type=MESH,
         )
 
     def extra_copy(j):
-        to = near_offset(j)
         return pltpu.make_async_remote_copy(
-            src_ref=extra.at[to % near],
+            src_ref=extra.at[near_index(j)],
             dst_ref=got_extra.at[j],
             send_sem=extra_send.at[0],
             recv_sem=extra_recv.at[0],
-            device_id=place(to),
+            device_id=near_place(j),
             device_id_type=MESH,
         )
 
@@ -210,13 +213,12 @@
     for l in range(slots):
         flat[pl.ds(l, groups, stride=slots), :] = live_rows[:, l * LANES : (l + 1) * LANES]
     inputs[1].wait()
-    targets = target_ref[...].astype(jnp.float32)
+    marked_targets = jnp.where(flat[...] > 0.0, target_ref[...].astype(jnp.float32), UNUSED)
     for k in range(count):
-        rows = slice(k * halves, (k + 1) * halves)
         from_me = (k // near + wings - wing) % wings if wings > 1 else 0
-        extra[k % near, from_me] = jnp.concatenate([flat[rows, :], targets[rows]], axis=0).astype(
-            jnp.bfloat16
-        )
+        for h in range(halves):
+            row = k * halves + h
+            extra[k % near, from_me, h : h + 1] = marked_targets[row : row + 1].astype(jnp.bfloat16)
     pltpu.make_async_copy(extra.at[me % near], got_extra.at[0], extra_recv.at[0]).start()
 
     pl.semaphore_wait(barrier, near - 1 + wing)
@@ -227,20 +229,11 @@
             pl.semaphore_signal(ready, inc=1, device_id=partner, device_id_type=MESH)
 
 
-    def send_feats(q):
-        def send(j, _):
+    for j in range(1, near):
+        extra_copy(j).start()
+    for q in range(len(kinds)):
+        for j in range(1, near):
             feat_copy(q, j).start()
-            return 0
-
-        lax.fori_loop(1, near, send, 0, unroll=True)
-
-    def send_extra(j, _):
-        extra_copy(j).start()
-        return 0
-
-    lax.fori_loop(1, near, send_extra, 0, unroll=True)
-    for q in range(len(kinds)):
-        send_feats(q)
     voxel_copy.wait()
     inputs[2].wait()
     inputs[3].wait()
@@ -282,7 +275,7 @@
             dst_ref=ref,
             send_sem=feat_send.at[0],
             recv_sem=sem,
-            device_id=place(at_offset(1)),
+            device_id=near_place(1),
             device_id_type=MESH,
         )
 
@@ -296,8 +289,9 @@
             more = jnp.concatenate(
                 [got_extra[g * group + u, w].astype(jnp.float32) for u in range(group)], axis=1
             )
-            live = jnp.where(along, more[h : h + 1], 0.0)
-            marked = live * more[halves + h : halves + h + 1]
+            target = more[h : h + 1]
+            live = jnp.where(along & (target < UNUSED), 1.0, 0.0)
+            marked = live * target
             left = jnp.concatenate(
                 [x * live[i : i + 1].astype(jnp.bfloat16) for i in range(tall)]
                 + [marked.astype(jnp.bfloat16)],
@@ -403,7 +397,23 @@
 
             if h + 1 == halves:
                 far_gather.start()
-            far_moments(h).start()
+
+            @pl.when(last_wing)
+            def _():
+                far_moments(h).start()
+
+            if h in [0]:
+
+                @pl.when(first_wing)
+                def _():
+                    far_moments(h).start()
+
+        elif wings > 1 and h in {1: [1]}:
+
+            @pl.when(first_wing)
+            def _():
+                for e in {1: [1]}[h]:
+                    far_moments(e).start()
 
     def unpack(ref, rows):
         for e in range(side):
@@ -448,23 +458,19 @@
             )
         unpack(my_ref, mz_ref[...])
 
-    def begin(t, _):
-        z_ref[0, at(t), :] = jnp.sum(block(square, t) * gathered(t), axis=1)
-        return 0
-
-    lax.fori_loop(0, chunks, begin, 0, unroll=True)
-
     here = [ix > 0, ix < gx - 1, iy > 0, iy < gy - 1]
     beside = [(ix - 1, iy), (ix + 1, iy), (ix, iy - 1), (ix, iy + 1)]
 
     def halo_copy(step, k):
         if k < 2:
-            source = z_ref.at[step, pl.ds(k * (bricks - 8), 8)]
+            source = z_ref.at[step, pl.ds(k * (bricks - BY), BY)]
+            target = halo.at[step, k ^ 1, pl.ds(0, BY)]
         else:
             source = y_send.at[step, k - 2]
+            target = halo.at[step, k ^ 1]
         return pltpu.make_async_remote_copy(
             src_ref=source,
-            dst_ref=halo.at[step, k ^ 1],
+            dst_ref=target,
             send_sem=halo_send.at[k],
             recv_sem=halo_recv.at[step % 2, k ^ 1],
             device_id=beside[k],
@@ -473,21 +479,41 @@
 
     def halo_arrived(step, k):
         return pltpu.make_async_remote_copy(
-            src_ref=y_send.at[step, 0],
-            dst_ref=halo.at[step, k],
+            src_ref=halo.at[step, k, pl.ds(0, BY if k < 2 else BX)],
+            dst_ref=halo.at[step, k, pl.ds(0, BY if k < 2 else BX)],
             send_sem=halo_send.at[k],
             recv_sem=halo_recv.at[step % 2, k],
             device_id=beside[k],
             device_id_type=MESH,
         )
 
+    def send_halos(step, ks):
+        for k in ks:
+
+            @pl.when(here[k])
+            def _():
+                halo_copy(step, k).start()
+
+    def produce(step, make):
+        for t in (0, chunks - 1):
+            z_ref[step, at(t), :] = make(t)
+        send_halos(step, (0, 1))
+        for t in range(1, chunks - 1):
+            z_ref[step, at(t), :] = make(t)
+        for e in range(2):
+            y_send[step, e] = z_ref[step, pl.ds(e * (BY - 1), BX, stride=BY), :]
+        send_halos(step, (2, 3))
+
+    produce(0, lambda t: jnp.sum(block(square, t) * gathered(t), axis=1))
+
     def part_copy(j):
+        a, b = divmod(j, gy)
         return pltpu.make_async_remote_copy(
             src_ref=part,
             dst_ref=parts.at[j],
             send_sem=part_send.at[0],
             recv_sem=part_recv.at[0],
-            device_id=place(at_offset(j)),
+            device_id=(all_rows_at[a], across_at[b]),
             device_id_type=MESH,
         )
 
@@ -497,7 +523,7 @@
             dst_ref=ref,
             send_sem=sem,
             recv_sem=part_recv.at[0],
-            device_id=place(at_offset(1)),
+            device_id=near_place(1),
             device_id_type=MESH,
         ).wait_send()
 
@@ -514,14 +540,6 @@
         return SCALE * (back + shifted)
 
     def operate(step):
-        for e in range(2):
-            y_send[step, e] = z_ref[step, pl.ds(e * (BY - 1), BX, stride=BY), :]
-        for k in range(4):
-
-            @pl.when(here[k])
-            def _():
-                halo_copy(step, k).start()
-
         def widen(t, _):
             made = next_basis(step, t)
             basis[step, at(t), :] = made
@@ -552,7 +570,7 @@
                 halo_arrived(step, k).wait_recv()
                 halo_copy(step, k).wait_send()
 
-        xm = jnp.concatenate([halo[step, 0][8 - BY :], z[: bricks - BY]], axis=0)
+        xm = jnp.concatenate([halo[step, 0][:BY], z[: bricks - BY]], axis=0)
         xp = jnp.concatenate([z[BY:], halo[step, 1][:BY]], axis=0)
         ym_ref[pl.ds(0, BX, stride=BY), :] = halo[step, 2]
         yp_ref[pl.ds(BY - 1, BX, stride=BY), :] = halo[step, 3]
@@ -563,13 +581,12 @@
 
         if step + 1 < ITERS:
 
-            def advance(t, _):
+            def advance(t):
                 back = jnp.sum(block(square, t) * as_column(mid_ref[at(t), :]), axis=1)
                 shifted = q_ref[at(t), :] - SHIFTS[step] * z_ref[step, at(t), :]
-                z_ref[step + 1, at(t), :] = SCALE * (back + shifted)
-                return 0
-
-            lax.fori_loop(0, chunks, advance, 0, unroll=True)
+                return SCALE * (back + shifted)
+
+            produce(step + 1, advance)
         else:
             for e, (a, b) in enumerate(late):
                 e += len(early)
@@ -590,11 +607,8 @@
     part[...] = mine
     parts[0] = mine
 
-    def start(j, _):
+    for j in part_order:
         part_copy(j).start()
-        return 0
-
-    lax.fori_loop(1, count, start, 0, unroll=True)
 
     def last(t, _):
         basis[ITERS, at(t), :] = next_basis(ITERS, t)
@@ -670,7 +684,7 @@
     wings = 2 if gx % 2 == 0 else 1
     kept = bricks * feat * (feat + SUBLANES) // 2 // LANES
     near = count // wings
-    group = 8
+    group = 16
     while near % group:
         group //= 2
     vmem = pl.BlockSpec(memory_space=pltpu.VMEM)
@@ -683,8 +697,8 @@
         out_specs=(vmem,) * 5,
         scratch_shapes=[
             pltpu.VMEM((wings * cols // LANES, near, feat, LANES), jnp.bfloat16),
-            pltpu.VMEM((near, wings, 2 * cols // LANES, LANES), jnp.bfloat16),
-            pltpu.VMEM((near, wings, 2 * cols // LANES, LANES), jnp.bfloat16),
+            pltpu.VMEM((near, wings, cols // LANES, LANES), jnp.bfloat16),
+            pltpu.VMEM((near, wings, cols // LANES, LANES), jnp.bfloat16),
             pltpu.VMEM((kept, LANES), f32),
             pltpu.VMEM((kept, LANES), f32),
             pltpu.VMEM((bricks * feat // LANES, LANES), f32),

time: 32.7 us -> 31.6 us (0.966)
  Pallas kernels: 31.2 us -> 30.2 us
    pallas_call x1, Pallas kernels: 31.2 us -> 30.2 us  [shards(): pl.pallas_call(functools.partial(kernel, gx, gy), out_shape=(pltpu.VMEM((...]
where the time goes in v5:
time: 31.6 us; the launch traced here: 31.5 us
  Pallas kernels  30.2 us (96%)
  other arithmetic  0.67 us (2%)
  between operations  0.64 us (2%)
    pallas_call x1, Pallas kernels, shards(): pl.pallas_call(functools.partial(kernel, gx, gy), out_shape=(pltpu.VMEM((...  30.2 us
    sub x1, other arithmetic, shards(): return (answer + alpha * direction, res - alpha * image)  0.67 us

profile of v5, /device:TPU:0, one launch (start us, length us, event | category | flops | bytes accessed | tf_op | source)
XLA Modules:
  0.0 31.5 jit_solution(6651406137428819318)
XLA Ops:
  0.6 30.2 %shard_map.77 = (f32[32,512]{1,0:T(8,128)S(1)}, f32[32,512]{1,0:T(8,128)S(1)}, f32[32,512]{1,0:T(8,128)S(1)}, f32[32,512]{1,0:T(8,128)S(1)}, f32[1,512]{1,0:T(1,128)S(1)}) custom-call(bf16[32,8192]{1,0:T(8,128)(2,1)} %feats_hbm.1, bf16[64,128]{1,0:T(8,128)(2,1)} %bitcast.6, s32[8,1024]{1,0:T(8,128)} %bitcast.5, s32[4,32]{1,0:T(4,128)} %bitcast.7, ...), custom_call_target="tpu_custom_call" | custom-call | tf_op jit(solution)/shard_map/pallas_call | solution.py:693
  30.8 0.7 %multiply_subtract_fusion = (f32[32,512]{1,0:T(8,128)}, f32[32,512]{1,0:T(8,128)}) fusion(f32[32,512]{1,0:T(8,128)S(1)} %get-tuple-element.10, f32[32,512]{1,0:T(8,128)S(1)} %get-tuple-element.11, f32[512]{0:T(512)S(1)} %bitcast.4, f32[32,512]{1,0:T(8,128)S(1)} %get-tuple-element.7, f32[32,512]{1,0:T(8,128)S(1)} %get-tuple-element.9), kind=kLoop, calls=%fused_computation | loop fusion | flops 65536 | bytes 395264 | tf_op jit(solution)/shard_map/sub | solution.py:755

commit v6 on v5

--- a/solution.py
+++ b/solution.py
@@ -17,6 +17,10 @@
 MESH = pl.DeviceIdType.MESH
 STRIDE = 11
 SCALE = 2.0**-8
+WINGS = 2
+HOLD_BACK = True
+DIRECT_LAST = True
+DIRECT = (0,)
 UNUSED = 256.0
 SHIFTS = (8.0, 1.0, 4.0)
 
@@ -85,9 +89,10 @@
     feat = got.shape[2]
     total_bricks, slots = lists_ref.shape[1], lists_ref.shape[0]
     near = got.shape[1]
-    wings = count // near
-    first = me // near * near
-    group = near // feat_recv.shape[1]
+    wings = WINGS
+    wing = me // near
+    plane = near // 2
+    chunk = math.gcd(plane, CHUNK)
     bricks = reg_ref.shape[0]
     cols = bricks * slots
     halves = cols // LANES
@@ -96,31 +101,48 @@
     tall = per_half // side
 
     half_gx = gx // wings
-    first_x = ix // half_gx * half_gx
-    rows_at = [(ix - first_x + a) % half_gx for a in range(half_gx)]
+    deep = half_gx // 2
+    first_x = wing * half_gx
+    layer = ix // deep % 2
+    inner = (layer + wing) % 2
+    gives = inner * wing
+    takes = inner * (1 - wing)
+    relays = 1 - wing * (1 - inner)
+    rows_at = [
+        [first_x + (layer + p) % 2 * deep + (ix % deep + a) % deep for a in range(deep)]
+        for p in range(2)
+    ]
     across_at = [(iy + b) % gy for b in range(gy)]
     all_rows_at = [(ix + a) % gx for a in range(gx)]
-    step_by = STRIDE if math.gcd(STRIDE, near) == 1 else 1
-    offsets = [divmod(j * step_by % near, gy) for j in range(near)]
+    step_by = STRIDE if math.gcd(STRIDE, plane) == 1 else 1
+    offsets = [
+        (j // plane,) + divmod(j % plane * step_by % plane, gy) for j in range(near)
+    ]
     part_order = list(range(count - 1, 0, -1))
-    kinds = [(w, h) for w in reversed(range(wings)) for h in range(halves)]
+
+    def near_x(j):
+        p, a, _ = offsets[j]
+        return rows_at[p][a]
+
+    def near_y(j):
+        return across_at[offsets[j][2]]
 
     def near_index(j):
-        a, b = offsets[j]
-        return rows_at[a] * gy + across_at[b]
+        return (near_x(j) - first_x) * gy + near_y(j)
 
     def near_place(j):
-        a, b = offsets[j]
-        return (first_x + rows_at[a], across_at[b])
+        return (near_x(j), near_y(j))
+
+    def far_place(j):
+        return ((near_x(j) + half_gx) % gx, near_y(j))
 
     def columns(j, w, h):
-        start = ((first_x + w * half_gx) % gx * gy + near_index(j)) * cols + h * LANES
+        start = ((near_x(j) + w * half_gx) % gx * gy + near_y(j)) * cols + h * LANES
         return pl.ds(pl.multiple_of(start, LANES), LANES)
 
     barrier = pltpu.get_barrier_semaphore()
 
     partner = ((ix + half_gx) % gx, iy)
-    wing = me // near
     first_wing = wing == 0
     last_wing = wing == wings - 1
 
@@ -148,35 +170,56 @@
         def _():
             pl.semaphore_signal(barrier, inc=1, device_id=partner, device_id_type=MESH)
 
+        @pl.when(takes == 1)
+        def _():
+            for j in range(plane, near):
+                pl.semaphore_signal(
+                    barrier, inc=1, device_id=far_place(j), device_id_type=MESH
+                )
+
     inputs[2].start()
     inputs[3].start()
     voxel_copy = pltpu.make_async_copy(voxel_hbm, voxel, voxel_sem)
     voxel_copy.start()
-    for q, (w, h) in enumerate(kinds):
-        pltpu.make_async_copy(
-            feats_hbm.at[:, columns(0, w, h)], got.at[q, 0], feat_recv.at[q, 0]
-        ).start()
+    for h in range(halves):
+        for w in range(wings):
+            kind = h + (1 - w) * halves
+            pltpu.make_async_copy(
+                feats_hbm.at[:, columns(0, w, h)], got.at[kind, 0], feat_recv.at[2 * kind]
+            ).start()
     halo[...] = jnp.zeros_like(halo)
     acc[...] = jnp.zeros_like(acc)
     gather[...] = jnp.zeros_like(gather)
 
-    def feat_copy(q, j):
+    def feat_copy(w, h, j):
+        flip = gives if w and offsets[j][0] and h in DIRECT else 0
+        kind = h + (1 - w) * halves
         return pltpu.make_async_remote_copy(
-            src_ref=feats_hbm.at[:, columns(j, *kinds[q])],
-            dst_ref=got.at[q, j],
+            src_ref=feats_hbm.at[:, columns(j, w, h)],
+            dst_ref=got.at[kind + flip * 2 * halves, j],
             send_sem=feat_send.at[0],
-            recv_sem=feat_recv.at[q, j // group],
+            recv_sem=feat_recv.at[2 * kind + offsets[j][0] + flip * (4 * halves - h - 1)],
+            device_id=((near_x(j) + flip * half_gx) % gx, near_y(j)),
+            device_id_type=MESH,
+        )
+
+    def extra_copy(w, j):
+        return pltpu.make_async_remote_copy(
+            src_ref=extra.at[near_index(j), w],
+            dst_ref=got_extra.at[1 - w, j],
+            send_sem=extra_send.at[0],
+            recv_sem=extra_recv.at[offsets[j][0] if w else 3],
             device_id=near_place(j),
             device_id_type=MESH,
         )
 
-    def extra_copy(j):
+    def direct_extra_copy(j):
         return pltpu.make_async_remote_copy(
-            src_ref=extra.at[near_index(j)],
-            dst_ref=got_extra.at[j],
-            send_sem=extra_send.at[0],
-            recv_sem=extra_recv.at[0],
-            device_id=near_place(j),
+            src_ref=extra.at[near_index(j), 1],
+            dst_ref=got_extra.at[2, j],
+            send_sem=extra_send.at[1],
+            recv_sem=extra_recv.at[2],
+            device_id=far_place(j),
             device_id_type=MESH,
         )
 
@@ -219,21 +262,34 @@
         for h in range(halves):
             row = k * halves + h
             extra[k % near, from_me, h : h + 1] = marked_targets[row : row + 1].astype(jnp.bfloat16)
-    pltpu.make_async_copy(extra.at[me % near], got_extra.at[0], extra_recv.at[0]).start()
-
-    pl.semaphore_wait(barrier, near - 1 + wing)
+    for w in range(wings):
+        pltpu.make_async_copy(
+            extra.at[me % near, w], got_extra.at[1 - w, 0], extra_recv.at[0 if w else 3]
+        ).start()
+
+    pl.semaphore_wait(barrier, near - 1 + wing + gives * plane)
     if wings > 1:
 
         @pl.when(last_wing)
         def _():
             pl.semaphore_signal(ready, inc=1, device_id=partner, device_id_type=MESH)
 
-
     for j in range(1, near):
-        extra_copy(j).start()
-    for q in range(len(kinds)):
+        extra_copy(1, j).start()
+
+    @pl.when(gives == 1)
+    def _():
+        for j in range(plane, near):
+            direct_extra_copy(j).start()
+
+    for h in range(halves):
         for j in range(1, near):
-            feat_copy(q, j).start()
+            feat_copy(1, h, j).start()
+    for j in range(1, near):
+        extra_copy(0, j).start()
+    for h in range(halves):
+        for j in range(1, near):
+            feat_copy(0, h, j).start()
     voxel_copy.wait()
     inputs[2].wait()
     inputs[3].wait()
@@ -253,6 +309,7 @@
         return 0
 
     lax.fori_loop(0, bricks // 4, squares, 0)
+
     linked = jnp.where(adjacency_ref[...] >= 0, 1.0, 0.0)
     same_brick = lax.broadcasted_iota(jnp.int32, (bricks, bricks), 0) == lax.broadcasted_iota(
         jnp.int32, (bricks, bricks), 1
@@ -264,7 +321,7 @@
     masks = [w > 0.0 for w in weights]
     degree = weights[0] + weights[1] + weights[2] + weights[3]
 
-    span_all = group * LANES
+    span_all = chunk * LANES
     owner = (lax.broadcasted_iota(jnp.int32, (1, span_all), 1) // slots) % per_half
     across = [jnp.where(owner % side == j, 1.0, 0.0).astype(jnp.bfloat16) for j in range(side)]
     along = owner // side == lax.broadcasted_iota(jnp.int32, (16, span_all), 0)
@@ -279,17 +336,18 @@
             device_id_type=MESH,
         )
 
-    def absorb(q):
-        w, h = kinds[q]
+    def absorb(kind, p, w, h, role):
+        first_slot = p * plane
+        slots_of = pl.ds(first_slot, plane)
+        sem = 8 + h if kind >= 2 * halves else 2 * kind + p
+        arrived(got.at[kind, slots_of], feat_recv.at[sem]).wait_recv()
 
         def some(g, _):
-            mine = pl.ds(g * group, group)
-            arrived(got.at[q, mine], feat_recv.at[q, g]).wait_recv()
-            x = jnp.concatenate([got[q, g * group + u] for u in range(group)], axis=1)
-            more = jnp.concatenate(
-                [got_extra[g * group + u, w].astype(jnp.float32) for u in range(group)], axis=1
+            mine = [first_slot + g * chunk + u for u in range(chunk)]
+            x = jnp.concatenate([got[kind, u] for u in mine], axis=1)
+            target = jnp.concatenate(
+                [got_extra[role, u].astype(jnp.float32)[h : h + 1] for u in mine], axis=1
             )
-            target = more[h : h + 1]
             live = jnp.where(along & (target < UNUSED), 1.0, 0.0)
             marked = live * target
             left = jnp.concatenate(
@@ -305,7 +363,10 @@
             gather[w, h * tall : (h + 1) * tall, :] += found[LANES : LANES + tall]
             return 0
 
-        lax.fori_loop(0, near // group, some, 0)
+        if plane == chunk:
+            some(0, 0)
+        else:
+            lax.fori_loop(0, plane // chunk, some, 0)
 
     def far_copy(source, target, e):
         return pltpu.make_async_remote_copy(
@@ -384,36 +445,66 @@
     far_gather = far_copy(gather.at[1], gather_far, 1)
     all_far_moments = far_copy(acc_sent, acc_far, 0)
 
-    arrived(got_extra, extra_recv.at[0]).wait_recv()
-    for q, (w, h) in enumerate(kinds):
-        absorb(q)
-        if w:
-            pack(h)
-            if h == 0:
-
-                @pl.when(first_wing)
-                def _():
-                    pl.semaphore_wait(ready, 1)
-
-            if h + 1 == halves:
-                far_gather.start()
-
-            @pl.when(last_wing)
+    def extras_arrived(role, p, count_of, e):
+        arrived(got_extra.at[role, pl.ds(p * plane, count_of)], extra_recv.at[e]).wait_recv()
+
+    extras_arrived(0, 0, plane, 0)
+
+    extras_arrived(0, 1, plane, 1)
+
+    for h in range(halves):
+        absorb(h, 0, 1, h, 0)
+
+        if h in DIRECT:
+
+            @pl.when(relays == 1)
+            def _():
+                absorb(h, 1, 1, h, 0)
+
+        else:
+            absorb(h, 1, 1, h, 0)
+
+        pack(h)
+        if h == 0:
+
+            @pl.when(first_wing)
+            def _():
+                pl.semaphore_wait(ready, 1)
+
+        if h + 1 == halves:
+            far_gather.start()
+
+        @pl.when(last_wing)
+        def _():
+            far_moments(h).start()
+
+        if h + 1 < halves or not HOLD_BACK:
+
+            @pl.when(first_wing)
             def _():
                 far_moments(h).start()
 
-            if h in [0]:
-
-                @pl.when(first_wing)
-                def _():
-                    far_moments(h).start()
-
-        elif wings > 1 and h in {1: [1]}:
-
-            @pl.when(first_wing)
-            def _():
-                for e in {1: [1]}[h]:
-                    far_moments(e).start()
+    def absorb_direct():
+        @pl.when(takes == 1)
+        def _():
+            extras_arrived(2, 1, plane, 2)
+            for h in DIRECT:
+                absorb(2 * halves + h, 1, 0, h, 2)
+
+    if not DIRECT_LAST:
+        absorb_direct()
+    extras_arrived(1, 0, near, 3)
+    for h in range(halves):
+        for p in range(2):
+            absorb(halves + h, p, 0, h, 1)
+    if HOLD_BACK:
+
+        @pl.when(first_wing)
+        def _():
+            far_moments(halves - 1).start()
+
+    if DIRECT_LAST:
+        absorb_direct()
 
     def unpack(ref, rows):
         for e in range(side):
@@ -616,8 +707,13 @@
 
     lax.fori_loop(0, chunks, last, 0)
 
-    sent(got.at[:, pl.ds(1, near - 1)], feat_send.at[0])
-    sent(got_extra.at[pl.ds(1, near - 1)], extra_send.at[0])
+    sent(got.at[pl.ds(0, 2 * halves), pl.ds(1, near - 1)], feat_send.at[0])
+    sent(got_extra.at[pl.ds(0, 2), pl.ds(1, near - 1)], extra_send.at[0])
+
+    @pl.when(gives == 1)
+    def _():
+        sent(got_extra.at[2, pl.ds(plane, plane)], extra_send.at[1])
+
     if wings > 1:
         far_gather.wait_send()
         all_far_moments.wait_send()
@@ -681,12 +777,10 @@
     bricks, _, vox = voxel_feats.shape
     count = gx * gy
     cols = bricks * slots
-    wings = 2 if gx % 2 == 0 else 1
+    wings = WINGS
+    halves = cols // LANES
     kept = bricks * feat * (feat + SUBLANES) // 2 // LANES
     near = count // wings
-    group = 16
-    while near % group:
-        group //= 2
     vmem = pl.BlockSpec(memory_space=pltpu.VMEM)
     hbm = pl.BlockSpec(memory_space=pltpu.HBM)
     f32 = jnp.float32
@@ -696,8 +790,8 @@
         in_specs=[hbm] * 6,
         out_specs=(vmem,) * 5,
         scratch_shapes=[
-            pltpu.VMEM((wings * cols // LANES, near, feat, LANES), jnp.bfloat16),
-            pltpu.VMEM((near, wings, cols // LANES, LANES), jnp.bfloat16),
+            pltpu.VMEM((3 * halves, near, feat, LANES), jnp.bfloat16),
+            pltpu.VMEM((3, near, halves, LANES), jnp.bfloat16),
             pltpu.VMEM((near, wings, cols // LANES, LANES), jnp.bfloat16),
             pltpu.VMEM((kept, LANES), f32),
             pltpu.VMEM((kept, LANES), f32),
@@ -727,9 +821,9 @@
             pltpu.SemaphoreType.DMA,
             pltpu.SemaphoreType.DMA((4,)),
             pltpu.SemaphoreType.DMA((1,)),
-            pltpu.SemaphoreType.DMA((wings * cols // LANES, near // group)),
-            pltpu.SemaphoreType.DMA((1,)),
-            pltpu.SemaphoreType.DMA((1,)),
+            pltpu.SemaphoreType.DMA((5 * halves,)),
+            pltpu.SemaphoreType.DMA((2,)),
+            pltpu.SemaphoreType.DMA((4,)),
             pltpu.SemaphoreType.DMA((2,)),
             pltpu.SemaphoreType.DMA((2,)),
             pltpu.SemaphoreType.DMA((4,)),

time: 31.6 us -> 31.3 us (level)
  Pallas kernels: 30.2 us -> 29.8 us
    pallas_call x1, Pallas kernels: 30.2 us -> 29.8 us  [shards(): pl.pallas_call(functools.partial(kernel, gx, gy), out_shape=(pltpu.VMEM((...]
where the time goes in v6:
time: 31.3 us; the launch traced here: 31.1 us
  Pallas kernels  29.8 us (95%)
  other arithmetic  0.67 us (2%)
  between operations  0.64 us (2%)
    pallas_call x1, Pallas kernels, shards(): pl.pallas_call(functools.partial(kernel, gx, gy), out_shape=(pltpu.VMEM((...  29.8 us
    sub x1, other arithmetic, shards(): return (answer + alpha * direction, res - alpha * image)  0.67 us

profile of v6, /device:TPU:0, one launch (start us, length us, event | category | flops | bytes accessed | tf_op | source)
XLA Modules:
  0.0 31.1 jit_solution(13869770654485313593)
XLA Ops:
  0.6 29.8 %shard_map.77 = (f32[32,512]{1,0:T(8,128)S(1)}, f32[32,512]{1,0:T(8,128)S(1)}, f32[32,512]{1,0:T(8,128)S(1)}, f32[32,512]{1,0:T(8,128)S(1)}, f32[1,512]{1,0:T(1,128)S(1)}) custom-call(bf16[32,8192]{1,0:T(8,128)(2,1)} %feats_hbm.1, bf16[64,128]{1,0:T(8,128)(2,1)} %bitcast.6, s32[8,1024]{1,0:T(8,128)} %bitcast.5, s32[4,32]{1,0:T(4,128)} %bitcast.7, ...), custom_call_target="tpu_custom_call" | custom-call | tf_op jit(solution)/shard_map/pallas_call | solution.py:787
  30.5 0.7 %multiply_subtract_fusion = (f32[32,512]{1,0:T(8,128)}, f32[32,512]{1,0:T(8,128)}) fusion(f32[32,512]{1,0:T(8,128)S(1)} %get-tuple-element.10, f32[32,512]{1,0:T(8,128)S(1)} %get-tuple-element.11, f32[512]{0:T(512)S(1)} %bitcast.4, f32[32,512]{1,0:T(8,128)S(1)} %get-tuple-element.7, f32[32,512]{1,0:T(8,128)S(1)} %get-tuple-element.9), kind=kLoop, calls=%fused_computation | loop fusion | flops 65536 | bytes 395264 | tf_op jit(solution)/shard_map/sub | solution.py:849

commit v7 on v6

--- a/solution.py
+++ b/solution.py
@@ -368,12 +368,12 @@
         else:
             lax.fori_loop(0, plane // chunk, some, 0)
 
-    def far_copy(source, target, e):
+    def far_copy(source, target, e, arrival):
         return pltpu.make_async_remote_copy(
             src_ref=source,
             dst_ref=target,
             send_sem=far_send.at[e],
-            recv_sem=far_recv.at[e],
+            recv_sem=far_recv.at[arrival],
             device_id=partner,
             device_id_type=MESH,
         )
@@ -440,10 +440,10 @@
     def far_moments(h):
         half = acc_sent.shape[0] // halves
         rows = pl.ds(h * half, half)
-        return far_copy(acc_sent.at[rows], acc_far.at[rows], 0)
-
-    far_gather = far_copy(gather.at[1], gather_far, 1)
-    all_far_moments = far_copy(acc_sent, acc_far, 0)
+        return far_copy(acc_sent.at[rows], acc_far.at[rows], 0, 1 + h)
+
+    far_gather = far_copy(gather.at[1], gather_far, 1, 0)
+    all_far_moments = far_copy(acc_sent, acc_far, 0, 1)
 
     def extras_arrived(role, p, count_of, e):
         arrived(got_extra.at[role, pl.ds(p * plane, count_of)], extra_recv.at[e]).wait_recv()
@@ -464,7 +464,6 @@
         else:
             absorb(h, 1, 1, h, 0)
 
-        pack(h)
         if h == 0:
 
             @pl.when(first_wing)
@@ -473,6 +472,7 @@
 
         if h + 1 == halves:
             far_gather.start()
+        pack(h)
 
         @pl.when(last_wing)
         def _():
@@ -497,11 +497,11 @@
     for h in range(halves):
         for p in range(2):
             absorb(halves + h, p, 0, h, 1)
-    if HOLD_BACK:
-
-        @pl.when(first_wing)
-        def _():
-            far_moments(halves - 1).start()
+        if HOLD_BACK and h == 0:
+
+            @pl.when(first_wing)
+            def _():
+                far_moments(halves - 1).start()
 
     if DIRECT_LAST:
         absorb_direct()
@@ -536,8 +536,8 @@
     def gathered(t):
         return as_column(g_ref[at(t), :])
 
-    def moments_times(step):
-        for t in range(chunks):
+    def moments_times(step, part_of):
+        for t in part_of:
             z_column = as_column(z_ref[step, at(t), :]).reshape(CHUNK // side, side, feat, 1)
             spread_column = z_column[:, 0]
             for e in range(1, side):
@@ -547,7 +547,6 @@
             mz_ref[t * (CHUNK // side) : (t + 1) * (CHUNK // side), :] = jnp.sum(
                 packed * spread_column, axis=1
             )
-        unpack(my_ref, mz_ref[...])
 
     here = [ix > 0, ix < gx - 1, iy > 0, iy < gy - 1]
     beside = [(ix - 1, iy), (ix + 1, iy), (ix, iy - 1), (ix, iy + 1)]
@@ -641,11 +640,13 @@
             return 0
 
         lax.fori_loop(0, chunks, widen, 0)
-        if step == 0 and wings > 1:
-            all_far_moments.wait_recv()
-            for h in range(halves):
+        each = chunks // halves
+        for h in range(halves):
+            if step == 0:
+                far_moments(h).wait_recv()
                 unpack_far(h)
-        moments_times(step)
+            moments_times(step, range(h * each, (h + 1) * each))
+        unpack(my_ref, mz_ref[...])
         z = z_ref[step]
         ym_ref[1:bricks, :] = z[: bricks - 1]
         yp_ref[0 : bricks - 1, :] = z[1:]
@@ -825,7 +826,7 @@
             pltpu.SemaphoreType.DMA((2,)),
             pltpu.SemaphoreType.DMA((4,)),
             pltpu.SemaphoreType.DMA((2,)),
-            pltpu.SemaphoreType.DMA((2,)),
+            pltpu.SemaphoreType.DMA((1 + halves,)),
             pltpu.SemaphoreType.DMA((4,)),
             pltpu.SemaphoreType.DMA((2, 4)),
             pltpu.SemaphoreType.DMA((1,)),

time: 31.3 us -> 31.3 us (level)
  no operation moved by 1% of the time
where the time goes in v7:
time: 31.3 us; the launch traced here: 31.1 us
  Pallas kernels  29.8 us (95%)
  other arithmetic  0.67 us (2%)
  between operations  0.64 us (2%)
    pallas_call x1, Pallas kernels, shards(): pl.pallas_call(functools.partial(kernel, gx, gy), out_shape=(pltpu.VMEM((...  29.8 us
    sub x1, other arithmetic, shards(): return (answer + alpha * direction, res - alpha * image)  0.67 us

profile of v7, /device:TPU:0, one launch (start us, length us, event | category | flops | bytes accessed | tf_op | source)
XLA Modules:
  0.0 31.1 jit_solution(12725899360314327608)
XLA Ops:
  0.6 29.8 %shard_map.77 = (f32[32,512]{1,0:T(8,128)S(1)}, f32[32,512]{1,0:T(8,128)S(1)}, f32[32,512]{1,0:T(8,128)S(1)}, f32[32,512]{1,0:T(8,128)S(1)}, f32[1,512]{1,0:T(1,128)S(1)}) custom-call(bf16[32,8192]{1,0:T(8,128)(2,1)} %feats_hbm.1, bf16[64,128]{1,0:T(8,128)(2,1)} %bitcast.6, s32[8,1024]{1,0:T(8,128)} %bitcast.5, s32[4,32]{1,0:T(4,128)} %bitcast.7, ...), custom_call_target="tpu_custom_call" | custom-call | tf_op jit(solution)/shard_map/pallas_call | solution.py:788
  30.5 0.7 %multiply_subtract_fusion = (f32[32,512]{1,0:T(8,128)}, f32[32,512]{1,0:T(8,128)}) fusion(f32[32,512]{1,0:T(8,128)S(1)} %get-tuple-element.10, f32[32,512]{1,0:T(8,128)S(1)} %get-tuple-element.11, f32[512]{0:T(512)S(1)} %bitcast.4, f32[32,512]{1,0:T(8,128)S(1)} %get-tuple-element.7, f32[32,512]{1,0:T(8,128)S(1)} %get-tuple-element.9), kind=kLoop, calls=%fused_computation | loop fusion | flops 65536 | bytes 395264 | tf_op jit(solution)/shard_map/sub | solution.py:850

commit v8 on v7

--- a/solution.py
+++ b/solution.py
@@ -69,6 +69,8 @@
     lists_ref,
     adjacency_ref,
     reg_ref,
+    feats_ref,
+    feats_sem,
     voxel_sem,
     input_sem,
     feat_send,
@@ -162,6 +164,8 @@
     ]
     inputs[0].start()
     inputs[1].start()
+    feats_in = pltpu.make_async_copy(feats_hbm, feats_ref, feats_sem)
+    feats_in.start()
     for j in range(1, near):
         greet(j)
     if wings > 1:
@@ -195,7 +199,7 @@
         flip = gives if w and offsets[j][0] and h in DIRECT else 0
         kind = h + (1 - w) * halves
         return pltpu.make_async_remote_copy(
-            src_ref=feats_hbm.at[:, columns(j, w, h)],
+            src_ref=feats_ref.at[:, columns(j, w, h)],
             dst_ref=got.at[kind + flip * 2 * halves, j],
             send_sem=feat_send.at[0],
             recv_sem=feat_recv.at[2 * kind + offsets[j][0] + flip * (4 * halves - h - 1)],
@@ -282,6 +286,7 @@
         for j in range(plane, near):
             direct_extra_copy(j).start()
 
+    feats_in.wait()
     for h in range(halves):
         for j in range(1, near):
             feat_copy(1, h, j).start()
@@ -819,6 +824,8 @@
             pltpu.VMEM((slots, brick_total), jnp.int32),
             pltpu.VMEM((4, bricks), jnp.int32),
             pltpu.VMEM((bricks, vox), f32),
+            pltpu.VMEM(point_feats.shape, point_feats.dtype),
+            pltpu.SemaphoreType.DMA,
             pltpu.SemaphoreType.DMA,
             pltpu.SemaphoreType.DMA((4,)),
             pltpu.SemaphoreType.DMA((1,)),

time: 31.3 us -> 31.1 us (level)
  no operation moved by 1% of the time
where the time goes in v8:
time: 31.1 us; the launch traced here: 30.9 us
  Pallas kernels  29.6 us (95%)
  other arithmetic  0.67 us (2%)
  between operations  0.64 us (2%)
    pallas_call x1, Pallas kernels, shards(): pl.pallas_call(functools.partial(kernel, gx, gy), out_shape=(pltpu.VMEM((...  29.6 us
    sub x1, other arithmetic, shards(): return (answer + alpha * direction, res - alpha * image)  0.67 us

profile of v8, /device:TPU:0, one launch (start us, length us, event | category | flops | bytes accessed | tf_op | source)
XLA Modules:
  0.0 30.9 jit_solution(3461017308833660375)
XLA Ops:
  0.6 29.6 %shard_map.77 = (f32[32,512]{1,0:T(8,128)S(1)}, f32[32,512]{1,0:T(8,128)S(1)}, f32[32,512]{1,0:T(8,128)S(1)}, f32[32,512]{1,0:T(8,128)S(1)}, f32[1,512]{1,0:T(1,128)S(1)}) custom-call(bf16[32,8192]{1,0:T(8,128)(2,1)} %feats_hbm.1, bf16[64,128]{1,0:T(8,128)(2,1)} %bitcast.6, s32[8,1024]{1,0:T(8,128)} %bitcast.5, s32[4,32]{1,0:T(4,128)} %bitcast.7, ...), custom_call_target="tpu_custom_call" | custom-call | tf_op jit(solution)/shard_map/pallas_call | solution.py:793
  30.3 0.7 %multiply_subtract_fusion = (f32[32,512]{1,0:T(8,128)}, f32[32,512]{1,0:T(8,128)}) fusion(f32[32,512]{1,0:T(8,128)S(1)} %get-tuple-element.10, f32[32,512]{1,0:T(8,128)S(1)} %get-tuple-element.11, f32[512]{0:T(512)S(1)} %bitcast.4, f32[32,512]{1,0:T(8,128)S(1)} %get-tuple-element.7, f32[32,512]{1,0:T(8,128)S(1)} %get-tuple-element.9), kind=kLoop, calls=%fused_computation | loop fusion | flops 65536 | bytes 395264 | tf_op jit(solution)/shard_map/sub | solution.py:857
